TPU v7x, 32 devices: a whole 2x2x4 slice. The times are simulated.
32 devices in a mesh: pairs: 2 (over x), tgt: 16 (over z, y, core).
Axes of the slice: x: 2, y: 2, z: 4, core: 2. Of those that a mesh axis runs over, the one named last changes fastest.
Arguments:
- source_features: bfloat16 [256, 1024], P(('pairs', 'tgt')), parts along dimension 0, may hold values from -6 to 6
- target_features: bfloat16 [64, 128, 1024], P(('pairs', 'tgt')), parts along dimension 0, may hold values from -6 to 6
- conv_first: float32 [16, 3, 3, 3, 3], replicated, may hold values from -2 to 2
- conv_second: float32 [16, 3, 3, 3, 3], replicated, may hold values from -0.625 to 0.625
Outputs:
- filtered: float32 [2, 128, 32, 128], P('pairs', None, 'tgt'), parts along dimension 0
There are 2 independent parts, one for each index of `pairs`. A program takes and returns all parts, laid end to end along the dimension named above; an argument that names none is the same for every part. Nothing has to cross between parts.
All inputs are finite; a program needn't handle non-finite values.
Results may differ from a plain program's by a relative error of at most 0.0028.
Values may be sent and summed in bfloat16 or wider, within the bound.
No kernel may reach another device: no remote copies, remote signals or barrier semaphores. Data moves between devices by JAX's collectives and lax.ppermute only.
A program may use at most 128 MiB of HBM per device.

v0:
```python
import functools

import jax
import jax.numpy as jnp
import numpy as np
from jax import lax
from jax.experimental import pallas as pl
from jax.experimental.pallas import tpu as pltpu
from jax.sharding import PartitionSpec as P

EPSILON = 1e-05
F32 = jnp.float32
BF16 = jnp.bfloat16
TAPS = 27
TAP_PAD = 32
SUBLANES = 8
ORDER = ((0, 0), (1, 0), (2, 0), (0, 1), (1, 1), (2, 1))
REPEATED = 4


def parts_of(local):
    hidden = local + 2
    count = -(-hidden // (SUBLANES - 2))
    size = -(-hidden // count)
    parts = []
    for start in range(0, hidden, size):
        first = min(start, max(0, local + 4 - SUBLANES))
        parts.append((first, start, min(size, hidden - start)))
    return parts


def first_selector(parts):
    tile = len(ORDER) * SUBLANES
    width = 3 * (tile + REPEATED * SUBLANES)
    blocks = [(first, hidden) for first, start, size in parts for hidden in range(start, start + size)]
    select = np.zeros((2 * TAP_PAD, len(blocks), width), np.float32)
    for number, (first, hidden) in enumerate(blocks):
        for b in range(3):
            for c in range(3):
                for d in range(3):
                    tap = (b * 3 + c) * 3 + d
                    for place, (offset, low) in enumerate(ORDER):
                        if offset != d:
                            continue
                        row = place * SUBLANES + hidden + b - first
                        select[tap, number, c * tile + row] = 1
                        if not low:
                            column = 3 * tile + c * REPEATED * SUBLANES + row
                            select[TAP_PAD + tap, number, column] = 1
    return select.reshape(2 * TAP_PAD, -1)


def second_selector(local):
    select = np.zeros((3, 3, 2, SUBLANES, local + 2, 2, TAP_PAD), np.float32)
    for b in range(3):
        for c in range(3):
            for d in range(3):
                tap = (b * 3 + c) * 3 + d
                for branch in range(2):
                    for cell in range(local):
                        select[c, d, branch, cell, cell + b, branch, tap] = 1
    return select.reshape(18 * SUBLANES, -1)


def unit(features):
    positive = jnp.maximum(features.astype(F32), 0.0)
    length = jnp.sqrt(jnp.sum(positive * positive, axis=-1, keepdims=True) + 1e-06)
    return (positive / length).astype(BF16)


def split(value):
    high = value.astype(BF16)
    return high, (value - high.astype(F32)).astype(BF16)


def prepare_kernel(
    hid, edge_ref, target_ref, first_ref, second_ref, pick_ref, spread_ref,
    unit_ref, first_out, second_out,
):
    rows, columns = target_ref.shape[:2]
    for row in range(rows):
        unit_ref[row * columns : (row + 1) * columns] = unit(target_ref[row])
    width = first_out.shape[1]
    taps = jnp.concatenate(split(first_ref[...]), axis=1)
    blocks = first_out.shape[0] // (2 * hid)
    for block in range(blocks):
        piece = jnp.dot(
            taps, pick_ref[:, block * width : (block + 1) * width], preferred_element_type=F32
        )
        if block == 0:
            piece = piece * edge_ref[0]
        if block == blocks - 1:
            piece = piece * edge_ref[1]
        first_out[block * 2 * hid : (block + 1) * 2 * hid] = piece.astype(BF16)
    depth = blocks * 2 * hid
    groups = blocks * 2
    row_group = lax.broadcasted_iota(jnp.int32, (groups * TAP_PAD, depth), 0) // TAP_PAD
    lane_group = lax.broadcasted_iota(jnp.int32, (groups * TAP_PAD, depth), 1) // hid
    tiled = jnp.concatenate([second_ref[...]] * groups, axis=0)
    tiled = jnp.where(row_group == lane_group, tiled, 0.0)
    high, low = split(tiled)
    half = second_out.shape[0] // 2
    high = jnp.dot(spread_ref[...], high, preferred_element_type=F32).astype(BF16)
    low = jnp.dot(spread_ref[...], low, preferred_element_type=F32).astype(BF16)
    second_out[:half, :depth] = high
    second_out[:half, depth:] = high
    second_out[half:, :depth] = low
    second_out[half:, depth:] = jnp.zeros_like(low)


def match_kernel(
    local, source_ref, target_ref, send_ref, order_ref
):
    rows, padded, columns = order_ref.shape
    cells = padded - 2 * SUBLANES
    correlation = lax.dot_general(
        unit(source_ref[...]), target_ref[...], (((1,), (1,)), ((), ())), preferred_element_type=F32
    )
    window = max(SUBLANES, local + 4)
    blank = jnp.zeros((SUBLANES, columns), F32)
    for row in range(rows):
        order_ref[row, :SUBLANES, :] = blank
        order_ref[row, SUBLANES + cells :, :] = blank
        order_ref[row, SUBLANES : SUBLANES + cells, :] = correlation[
            :, row * columns : (row + 1) * columns
        ]
        source_best = jnp.max(order_ref[row], axis=0, keepdims=True)
        inverse = 1.0 / (source_best + EPSILON)
        for target in range(send_ref.shape[0]):
            first = SUBLANES + target * local - 2
            send_ref[target, row * window : (row + 1) * window] = order_ref[
                row, first : first + window, :
            ]
            place = rows * window + row
            send_ref[target, place : place + 1] = inverse


def lane_shifts(value):
    lanes = value.shape[-1]
    lane = lax.broadcasted_iota(jnp.int32, value.shape, value.ndim - 1)
    axis = value.ndim - 1
    left = jnp.where(lane == 0, 0.0, pltpu.roll(value, 1, axis))
    right = jnp.where(lane == lanes - 1, 0.0, pltpu.roll(value, lanes - 1, axis))
    return left, right


def consensus_kernel(
    parts, local, rows, came_ref, first_ref, second_ref, send_ref, tile_ref, partial_ref
):
    devices, _, columns = came_ref.shape
    window = max(SUBLANES, local + 4)
    grid_rows = devices * rows
    tile = len(ORDER) * SUBLANES
    again = REPEATED * SUBLANES
    zero = jnp.zeros((SUBLANES, columns), F32)

    def piece_of(device, row, first):
        return came_ref[device, row * window + first : row * window + first + SUBLANES, :]

    def survey(device, best):
        best = list(best)
        for number, (first, _, _) in enumerate(parts):
            for row in range(rows):
                best[number] = jnp.maximum(best[number], piece_of(device, row, first))
        return tuple(best)

    best = lax.fori_loop(0, devices, survey, (zero,) * len(parts), unroll=4)
    scales = [
        jnp.broadcast_to(1.0 / (jnp.max(most, axis=1, keepdims=True) + EPSILON), most.shape)
        for most in best
    ]

    blank = jnp.zeros((tile, columns), BF16)
    for number in range(len(parts)):
        tile_ref[0, number] = blank
        tile_ref[grid_rows + 1, number] = blank

    def build(device, carry):
        for row in range(rows):
            place = rows * window + row
            inverse = came_ref[device, place : place + 1, :]
            for number, (first, _, _) in enumerate(parts):
                value = piece_of(device, row, first)
                value = value * (value * inverse) * (value * scales[number])
                left, right = lane_shifts(value)
                moved = (left, value, right)
                high = [piece.astype(BF16).astype(F32) for piece in moved]
                low = [piece - rounded for piece, rounded in zip(moved, high)]
                stacked = jnp.concatenate(
                    [(low if part else high)[offset] for offset, part in ORDER], axis=0
                )
                tile_ref[device * rows + row + 1, number] = stacked.astype(BF16)
        return carry

    lax.fori_loop(0, devices, build, 0, unroll=2)

    partial_rows = second_ref.shape[0] // 2
    empty = jnp.zeros((partial_rows, columns), F32)
    partial_ref[0] = empty
    partial_ref[grid_rows + 1] = empty
    sides = 2
    unroll = 2

    def layers(step, carry):
        for index in range(unroll):
            base = (step * unroll + index) * sides
            hidden = []
            offset = 0
            for number, (_, _, size) in enumerate(parts):
                taps = []
                for side in range(sides):
                    pieces = [tile_ref[base + side + c, number] for c in range(3)]
                    pieces += [tile_ref[base + side + c, number, :again] for c in range(3)]
                    taps.append(jnp.concatenate(pieces, axis=0))
                count = size * first_ref.shape[0] // (local + 2)
                hidden.append(
                    jnp.dot(
                        first_ref[offset : offset + count],
                        jnp.concatenate(taps, axis=1),
                        preferred_element_type=F32,
                    )
                )
                offset += count
            halves = [split(jnp.maximum(piece, 0.0)) for piece in hidden]
            pair = jnp.concatenate(
                [high for high, _ in halves] + [low for _, low in halves], axis=0
            )
            partial = jnp.dot(second_ref[...], pair, preferred_element_type=F32)
            partial = partial[:partial_rows] + partial[partial_rows:]
            for side in range(sides):
                partial_ref[base + side + 1] = partial[:, side * columns : (side + 1) * columns]
        return carry

    lax.fori_loop(0, grid_rows // (sides * unroll), layers, 0)

    def gather(device, most):
        for row in range(rows):
            total = None
            for branch in range(2):
                sums = []
                for d in range(3):
                    value = None
                    for c in range(3):
                        start = ((c * 3 + d) * 2 + branch) * SUBLANES
                        piece = partial_ref[device * rows + row + c, start : start + SUBLANES, :]
                        value = piece if value is None else value + piece
                    sums.append(value)
                output = lane_shifts(sums[0])[0] + sums[1] + lane_shifts(sums[2])[1]
                output = jnp.maximum(output, 0.0)
                total = output if total is None else total + output
            send_ref[device, row * SUBLANES : (row + 1) * SUBLANES] = total
            most = jnp.maximum(most, total)
        return most

    most = lax.fori_loop(0, devices, gather, zero, unroll=2)
    scale = jnp.broadcast_to(
        1.0 / (jnp.max(most, axis=1, keepdims=True) + EPSILON), most.shape
    )
    for device in range(devices):
        send_ref[device, rows * SUBLANES :] = scale


def finish_kernel(local, came_ref, out_ref):
    devices = came_ref.shape[0]
    rows = out_ref.shape[1]
    for row in range(rows):
        first = row * SUBLANES
        most = came_ref[0, first : first + SUBLANES]
        for device in range(1, devices):
            most = jnp.maximum(most, came_ref[device, first : first + SUBLANES])
        inverse = 1.0 / (jnp.max(most, axis=0, keepdims=True) + EPSILON)
        for device in range(devices):
            value = came_ref[device, first : first + SUBLANES]
            scale = came_ref[device, rows * SUBLANES :]
            value = value * (value * inverse) * (value * scale)
            out_ref[device * local : (device + 1) * local, row, :] = value[:local]


def exchange(slots):
    return lax.all_to_all(slots, "tgt", 0, 0, tiled=True)


def room(*shapes):
    scratch = sum(int(np.prod(shape)) * jnp.dtype(kind).itemsize for shape, kind in shapes)
    return pltpu.CompilerParams(vmem_limit_bytes=scratch + 6 * 2**20)


VMEM = pl.BlockSpec(memory_space=pltpu.VMEM)
SMEM = pl.BlockSpec(memory_space=pltpu.SMEM)


def shards(source_features, target_features, conv_first, conv_second):
    devices = lax.axis_size("tgt")
    position = lax.axis_index("tgt")
    rows, columns, channels = target_features.shape
    cells = source_features.shape[0] * devices
    hid = conv_first.shape[0]
    local = cells // devices
    parts = parts_of(local)
    hidden = local + 2
    window = max(SUBLANES, local + 4)
    tile = len(ORDER) * SUBLANES
    width = 3 * (tile + REPEATED * SUBLANES)
    depth = hidden * 2 * hid
    assert local <= SUBLANES and rows * devices % 4 == 0

    spread = jnp.broadcast_to(source_features[None], (devices,) + source_features.shape)
    sources = exchange(spread).reshape(cells, channels)

    direct = conv_first[:, 1].reshape(hid, TAPS)
    turned = jnp.transpose(conv_first[:, :, :, 1, :], (0, 3, 1, 2)).reshape(hid, TAPS)
    first_taps = jnp.pad(jnp.concatenate([direct, turned]), ((0, 0), (0, TAP_PAD - TAPS)))
    direct = conv_second[:, 1].reshape(hid, TAPS)
    turned = jnp.transpose(conv_second[:, :, :, 1, :], (0, 3, 1, 2)).reshape(hid, TAPS)
    second_taps = jnp.pad(jnp.concatenate([direct, turned]), ((0, 0), (0, TAP_PAD - TAPS)))
    second_taps = jnp.tile(second_taps.T, (1, hidden))
    edges = jnp.stack([position > 0, position < devices - 1]).astype(F32)
    second_rows = 18 * SUBLANES
    target_unit, first_weights, second_weights = pl.pallas_call(
        functools.partial(prepare_kernel, hid),
        out_shape=(
            jax.ShapeDtypeStruct((rows * columns, channels), BF16),
            jax.ShapeDtypeStruct((depth, width), BF16),
            jax.ShapeDtypeStruct((2 * second_rows, 2 * depth), BF16),
        ),
        in_specs=[SMEM] + [VMEM] * 5,
        out_specs=(VMEM,) * 3,
        cost_estimate=pl.CostEstimate(flops=10**6, bytes_accessed=2 * 10**6, transcendentals=0),
        compiler_params=room(),
        name="prepare",
    )(
        edges,
        target_features,
        first_taps,
        second_taps,
        jnp.asarray(first_selector(parts), BF16),
        jnp.asarray(second_selector(local), BF16),
    )

    slots = pl.pallas_call(
        functools.partial(match_kernel, local),
        out_shape=jax.ShapeDtypeStruct((devices, rows * window + rows, columns), F32),
        in_specs=[VMEM] * 2,
        out_specs=VMEM,
        scratch_shapes=[
            pltpu.VMEM((rows, cells + 2 * SUBLANES, columns), F32),
        ],
        compiler_params=room(),
        name="match",
    )(sources, target_unit)

    stores = (
        ((rows * devices + 2, len(parts), tile, columns), BF16),
        ((rows * devices + 2, second_rows, columns), F32),
    )
    slots = pl.pallas_call(
        functools.partial(consensus_kernel, parts, local, rows),
        out_shape=jax.ShapeDtypeStruct((devices, (rows + 1) * SUBLANES, columns), F32),
        in_specs=[VMEM] * 3,
        out_specs=VMEM,
        scratch_shapes=[pltpu.VMEM(shape, kind) for shape, kind in stores],
        compiler_params=room(*stores),
        name="consensus",
    )(exchange(slots), first_weights, second_weights)

    filtered = pl.pallas_call(
        functools.partial(finish_kernel, local),
        out_shape=jax.ShapeDtypeStruct((cells, rows, columns), F32),
        in_specs=[VMEM],
        out_specs=VMEM,
        compiler_params=room(),
        name="finish",
    )(exchange(slots))
    return filtered[None]


def solution(mesh):
    placed = (P(("pairs", "tgt"), None), P(("pairs", "tgt"), None, None), P(), P())
    return jax.shard_map(
        shards, mesh=mesh, in_specs=placed, out_specs=P("pairs", None, "tgt", None), check_vma=False
    )
```

profile of v0, /device:TPU:0, one launch (start us, length us, event | category | flops | bytes accessed | tf_op | source)
XLA Modules:
  0.0 51.0 jit_solution(3735804775921518212)
XLA Ops:
  0.0 1.4 %broadcast_in_dim.4 = bf16[16,8,1024]{2,1,0:T(8,128)(2,1)} broadcast(bf16[8,1024]{1,0:T(8,128)(2,1)} %param.6), dimensions={1,2} | broadcast | bytes 278528 | tf_op jit(solution)/shard_map/broadcast_in_dim | solution.py:307
  1.5 7.5 %all-to-all-start = ((bf16[16,8,1024]{2,1,0:T(8,128)(2,1)}), bf16[16,8,1024]{2,1,0:T(8,128)(2,1)S(1)}, u32[]{:S(2)}, u32[]{:S(2)}) async-start(bf16[16,8,1024]{2,1,0:T(8,128)(2,1)} %broadcast_in_dim.4), calls=%async_computation | async-start | bytes 524288 | tf_op jit(solution)/shard_map/all_to_all | solution.py:280
  9.0 0.0 copy-done.3
  9.0 0.0 slice-start
  9.0 0.0 copy-start.4
  9.1 0.0 copy-start
  9.1 0.1 copy.11
  9.2 0.6 %slice-done = f32[16,1,3,3,3]{0,4,3,2,1:T(4,128)S(1)} async-done(((f32[16,3,3,3,3]{0,4,3,2,1:T(4,128)}), f32[16,1,3,3,3]{0,4,3,2,1:T(4,128)S(1)}, s32[]{:S(2)}) %slice-start) | async-done | bytes 1752 | tf_op jit(solution)/shard_map/slice | solution.py:310
  9.8 0.1 copy.10
  9.8 0.0 copy-done.4
  9.9 0.0 slice-done.1
  9.9 0.1 fusion
  10.0 0.0 copy-start.2
  10.0 0.1 tile.10.second_ref
  10.1 0.1 add_convert_fusion.edge_ref
  10.2 0.8 %copy-done.1 = bf16[64,2400]{1,0:T(8,128)(2,1)S(1)} copy-done((bf16[64,2400]{1,0:T(8,128)(2,1)S(1)}, bf16[64,2400]{1,0:T(8,128)(2,1)}, u32[]{:S(2)}) %copy-start.1) | copy-done | bytes 307224
  11.0 0.0 copy-done.2
  11.0 1.2 %prepare.1 = (bf16[256,1024]{1,0:T(8,128)(2,1)S(1)}, bf16[320,240]{1,0:T(8,128)(2,1)S(1)}, bf16[288,640]{1,0:T(8,128)(2,1)S(1)}) custom-call(f32[2]{0:T(128)S(1)} %add_convert_fusion.edge_ref, bf16[2,128,1024]{2,1,0:T(8,128)(2,1)S(1)} %copy-done, f32[32,32]{1,0:T(8,128)S(1)} %select_maximum_fusion.1.first_ref, f32[32,320]{1,0:T(8,128)S(1)} %tile.10.second_ref, ...), custom_call_target="tpu_custom_call" | custom-call | flops 1000000 | bytes 2000000 | tf_op jit(solution)/shard_map/prepare/pallas_call | solution.py:319
  12.2 6.8 %all-to-all-done = bf16[16,8,1024]{2,1,0:T(8,128)(2,1)S(1)} async-done(((bf16[16,8,1024]{2,1,0:T(8,128)(2,1)}), bf16[16,8,1024]{2,1,0:T(8,128)(2,1)S(1)}, u32[]{:S(2)}, u32[]{:S(2)}) %all-to-all-start) | async-done | bytes 262176 | tf_op jit(solution)/shard_map/all_to_all | solution.py:280
  19.0 0.4 match.1
  19.4 12.7 %all_to_all.15.came_ref = f32[16,26,128]{2,1,0:T(8,128)S(1)} all-to-all(f32[16,26,128]{2,1,0:T(8,128)S(1)} %match.1), channel_id=1, replica_groups=mesh['pairs'=2,'tgt'=16] {'tgt'}, dimensions={0} | all-to-all | bytes 425984 | tf_op jit(solution)/shard_map/all_to_all | solution.py:280
  32.1 6.5 %consensus.1 = f32[16,24,128]{2,1,0:T(8,128)S(1)} custom-call(f32[16,26,128]{2,1,0:T(8,128)S(1)} %all_to_all.15.came_ref, bf16[320,240]{1,0:T(8,128)(2,1)S(1)} %get-tuple-element.9.first_ref, bf16[288,640]{1,0:T(8,128)(2,1)S(1)} %get-tuple-element.10.second_ref), custom_call_target="tpu_custom_call" | custom-call | tf_op jit(solution)/shard_map/consensus/pallas_call | solution.py:356
  38.6 11.6 %all_to_all.16.came_ref = f32[16,24,128]{2,1,0:T(8,128)S(1)} all-to-all(f32[16,24,128]{2,1,0:T(8,128)S(1)} %consensus.1), channel_id=1, replica_groups=mesh['pairs'=2,'tgt'=16] {'tgt'}, dimensions={0} | all-to-all | bytes 393216 | tf_op jit(solution)/shard_map/all_to_all | solution.py:280
  50.2 0.8 %finish.1 = f32[128,2,128]{2,1,0:T(2,128)} custom-call(f32[16,24,128]{2,1,0:T(8,128)S(1)} %all_to_all.16.came_ref), custom_call_target="tpu_custom_call" | custom-call | tf_op jit(solution)/shard_map/finish/pallas_call | solution.py:366
  (14 shorter events, 0.1 us)
Async XLA Ops:
  1.4 7.6 %copy-start.3 = (f32[16,3,3,3,3]{0,4,3,2,1:T(4,128)S(1)}, f32[16,3,3,3,3]{0,4,3,2,1:T(4,128)}, u32[]{:S(2)}) copy-start(f32[16,3,3,3,3]{0,4,3,2,1:T(4,128)} %param.8) | copy-start | bytes 15556
  1.5 8.4 %slice-start.1 = ((f32[16,3,3,3,3]{0,4,3,2,1:T(4,128)}), f32[16,1,3,3,3]{0,4,3,2,1:T(4,128)S(1)}, s32[]{:S(2)}) async-start(f32[16,3,3,3,3]{0,4,3,2,1:T(4,128)} %param.9), calls=%async_computation.4 | async-start | bytes 36864 | tf_op jit(solution)/shard_map/slice | solution.py:313
  1.5 17.6 %all-to-all-start = ((bf16[16,8,1024]{2,1,0:T(8,128)(2,1)}), bf16[16,8,1024]{2,1,0:T(8,128)(2,1)S(1)}, u32[]{:S(2)}, u32[]{:S(2)}) async-start(bf16[16,8,1024]{2,1,0:T(8,128)(2,1)} %broadcast_in_dim.4), calls=%async_computation | async-start | bytes 524288 | tf_op jit(solution)/shard_map/all_to_all | solution.py:280
  9.0 0.7 %slice-start = ((f32[16,3,3,3,3]{0,4,3,2,1:T(4,128)}), f32[16,1,3,3,3]{0,4,3,2,1:T(4,128)S(1)}, s32[]{:S(2)}) async-start(f32[16,3,3,3,3]{0,4,3,2,1:T(4,128)} %param.8), calls=%async_computation.3 | async-start | bytes 36864 | tf_op jit(solution)/shard_map/slice | solution.py:310
  9.0 0.8 %copy-start.4 = (f32[16,3,3,3,3]{0,4,3,2,1:T(4,128)S(1)}, f32[16,3,3,3,3]{0,4,3,2,1:T(4,128)}, u32[]{:S(2)}) copy-start(f32[16,3,3,3,3]{0,4,3,2,1:T(4,128)} %param.9) | copy-start | bytes 15556
  9.1 1.2 %copy-start = (bf16[2,128,1024]{2,1,0:T(8,128)(2,1)S(1)}, bf16[2,128,1024]{2,1,0:T(8,128)(2,1)}, u32[]{:S(2)}) copy-start(bf16[2,128,1024]{2,1,0:T(8,128)(2,1)} %target_ref.1) | copy-start | bytes 1572868
  10.0 1.0 %copy-start.1 = (bf16[64,2400]{1,0:T(8,128)(2,1)S(1)}, bf16[64,2400]{1,0:T(8,128)(2,1)}, u32[]{:S(2)}) copy-start(bf16[64,2400]{1,0:T(8,128)(2,1)} %constant.14.clone.pick_ref) | copy-start | bytes 921604
  10.0 1.0 %copy-start.2 = (bf16[144,640]{1,0:T(8,128)(2,1)S(1)}, bf16[144,640]{1,0:T(8,128)(2,1)}, u32[]{:S(2)}) copy-start(bf16[144,640]{1,0:T(8,128)(2,1)} %constant.15.clone.spread_ref) | copy-start | bytes 552964
where the time goes:
time: 51.4 us; the launch traced here: 51 us
  blocking collectives  24.3 us (47%)
  Pallas kernels  8.79 us (17%)
  starting transfers between devices  7.55 us (15%)
  waiting for transfers between devices  6.83 us (13%)
  local copies, waits for them, and re-layouts  3.2 us (6%)
    all_to_all x2, blocking collectives, exchange(): return lax.all_to_all(slots, 'tgt', 0, 0, tiled=True)  24.3 us
    all_to_all x1, starting transfers between devices, exchange(): return lax.all_to_all(slots, 'tgt', 0, 0, tiled=True)  7.55 us
    all_to_all x1, waiting for transfers between devices, exchange(): return lax.all_to_all(slots, 'tgt', 0, 0, tiled=True)  6.83 us
    pallas_call x1, Pallas kernels, shards(): pl.pallas_call(functools.partial(consensus_kernel, parts, local, rows), o...  6.48 us
    broadcast_in_dim x1, local copies, waits for them, and re-layouts, shards(): jnp.broadcast_to(source_features[None], (devices,) + source_features.shape)  1.45 us
    pallas_call x1, Pallas kernels, shards(): pl.pallas_call(functools.partial(prepare_kernel, hid), out_shape=(jax.Sha...  1.16 us
  transfers between devices with their start and end apart: 1, of which 1 were waited for; matrix products, arithmetic and copies ran while one was open for 1% of the time, Pallas kernels for 2%

commit v1 on v0

--- a/solution.py
+++ b/solution.py
@@ -11,7 +11,6 @@
 EPSILON = 1e-05
 F32 = jnp.float32
 BF16 = jnp.bfloat16
-TAPS = 27
 TAP_PAD = 32
 SUBLANES = 8
 ORDER = ((0, 0), (1, 0), (2, 0), (0, 1), (1, 1), (2, 1))
@@ -74,29 +73,46 @@
 
 
 def prepare_kernel(
-    hid, edge_ref, target_ref, first_ref, second_ref, pick_ref, spread_ref,
-    unit_ref, first_out, second_out,
+    devices, target_ref, first_ref, second_ref, pick_ref, spread_ref, gate_ref,
+    unit_ref, first_out, second_out, taps_ref,
 ):
     rows, columns = target_ref.shape[:2]
     for row in range(rows):
         unit_ref[row * columns : (row + 1) * columns] = unit(target_ref[row])
+    hid = first_ref.shape[-1]
+    taps_ref[...] = jnp.zeros(taps_ref.shape, F32)
+    for number, ref in enumerate((first_ref, second_ref)):
+        base = 2 * TAP_PAD * number
+        for b in range(3):
+            for c in range(3):
+                start = base + (b * 3 + c) * 3
+                taps_ref[start : start + 3, :hid] = ref[1, b, c]
+        for c in range(3):
+            for d in range(3):
+                piece = ref[c, d, 1]
+                for b in range(3):
+                    start = base + TAP_PAD + (b * 3 + c) * 3 + d
+                    taps_ref[start : start + 1, :hid] = piece[b : b + 1]
+    branches = [taps_ref[i * TAP_PAD : (i + 1) * TAP_PAD, :hid] for i in range(4)]
     width = first_out.shape[1]
-    taps = jnp.concatenate(split(first_ref[...]), axis=1)
+    taps = jnp.concatenate(split(jnp.concatenate(branches[:2], axis=1)), axis=0)
     blocks = first_out.shape[0] // (2 * hid)
     for block in range(blocks):
-        piece = jnp.dot(
-            taps, pick_ref[:, block * width : (block + 1) * width], preferred_element_type=F32
+        piece = lax.dot_general(
+            taps, pick_ref[:, block * width : (block + 1) * width],
+            (((0,), (0,)), ((), ())), preferred_element_type=F32,
         )
         if block == 0:
-            piece = piece * edge_ref[0]
+            piece = piece * jnp.where(lax.axis_index("tgt") == 0, 0.0, 1.0)
         if block == blocks - 1:
-            piece = piece * edge_ref[1]
+            piece = piece * jnp.where(lax.axis_index("tgt") == devices - 1, 0.0, 1.0)
         first_out[block * 2 * hid : (block + 1) * 2 * hid] = piece.astype(BF16)
     depth = blocks * 2 * hid
     groups = blocks * 2
     row_group = lax.broadcasted_iota(jnp.int32, (groups * TAP_PAD, depth), 0) // TAP_PAD
     lane_group = lax.broadcasted_iota(jnp.int32, (groups * TAP_PAD, depth), 1) // hid
-    tiled = jnp.concatenate([second_ref[...]] * groups, axis=0)
+    tiled = jnp.concatenate([jnp.concatenate(branches[2:], axis=1)] * blocks, axis=1)
+    tiled = jnp.concatenate([tiled] * groups, axis=0)
     tiled = jnp.where(row_group == lane_group, tiled, 0.0)
     high, low = split(tiled)
     half = second_out.shape[0] // 2
@@ -108,13 +124,52 @@
     second_out[half:, depth:] = jnp.zeros_like(low)
 
 
+def spread_kernel(
+    source_ref, target_ref, pick_ref, scatter_ref,
+    out_ref, target_out, pick_out, scatter_out, source_copy, sems,
+):
+    copies = [
+        pltpu.make_async_copy(start, end, sems.at[number])
+        for number, (start, end) in enumerate(
+            (
+                (source_ref, source_copy),
+                (target_ref, target_out),
+                (pick_ref, pick_out),
+                (scatter_ref, scatter_out),
+            )
+        )
+    ]
+    for copy in copies:
+        copy.start()
+    copies[0].wait()
+    half = out_ref.shape[2]
+    for device in range(out_ref.shape[0]):
+        start = device % 2 * half
+        out_ref[device] = source_copy[:, start : start + half]
+    for copy in copies[1:]:
+        copy.wait()
+
+
 def match_kernel(
-    local, source_ref, target_ref, send_ref, order_ref
+    local, mine_ref, other_ref, target_ref, send_ref, source_ref, order_ref
 ):
     rows, padded, columns = order_ref.shape
     cells = padded - 2 * SUBLANES
+    half = mine_ref.shape[1]
+    side = lax.axis_index("tgt") % 2
+    block = min(cells, 32)
+    for first in range(0, cells, block):
+        halves = [
+            jnp.maximum(ref[first : first + block].astype(F32), 0.0)
+            for ref in (mine_ref, other_ref)
+        ]
+        squares = [jnp.sum(piece * piece, axis=-1, keepdims=True) for piece in halves]
+        length = jnp.sqrt(squares[0] + squares[1] + 1e-06)
+        for number, piece in enumerate(halves):
+            start = pl.multiple_of((side ^ number) * half, half)
+            source_ref[first : first + block, pl.ds(start, half)] = (piece / length).astype(BF16)
     correlation = lax.dot_general(
-        unit(source_ref[...]), target_ref[...], (((1,), (1,)), ((), ())), preferred_element_type=F32
+        source_ref[...], target_ref[...], (((1,), (1,)), ((), ())), preferred_element_type=F32
     )
     window = max(SUBLANES, local + 4)
     blank = jnp.zeros((SUBLANES, columns), F32)
@@ -173,14 +228,14 @@
     blank = jnp.zeros((tile, columns), BF16)
     for number in range(len(parts)):
         tile_ref[0, number] = blank
-        tile_ref[grid_rows + 1, number] = blank
-
-    def build(device, carry):
+
+    def build(device, present):
+        source = jnp.minimum(device, devices - 1)
         for row in range(rows):
             place = rows * window + row
-            inverse = came_ref[device, place : place + 1, :]
+            inverse = came_ref[source, place : place + 1, :] * present
             for number, (first, _, _) in enumerate(parts):
-                value = piece_of(device, row, first)
+                value = piece_of(source, row, first)
                 value = value * (value * inverse) * (value * scales[number])
                 left, right = lane_shifts(value)
                 moved = (left, value, right)
@@ -190,48 +245,37 @@
                     [(low if part else high)[offset] for offset, part in ORDER], axis=0
                 )
                 tile_ref[device * rows + row + 1, number] = stacked.astype(BF16)
-        return carry
-
-    lax.fori_loop(0, devices, build, 0, unroll=2)
 
     partial_rows = second_ref.shape[0] // 2
     empty = jnp.zeros((partial_rows, columns), F32)
     partial_ref[0] = empty
     partial_ref[grid_rows + 1] = empty
-    sides = 2
-    unroll = 2
-
-    def layers(step, carry):
-        for index in range(unroll):
-            base = (step * unroll + index) * sides
-            hidden = []
-            offset = 0
-            for number, (_, _, size) in enumerate(parts):
-                taps = []
-                for side in range(sides):
-                    pieces = [tile_ref[base + side + c, number] for c in range(3)]
-                    pieces += [tile_ref[base + side + c, number, :again] for c in range(3)]
-                    taps.append(jnp.concatenate(pieces, axis=0))
-                count = size * first_ref.shape[0] // (local + 2)
-                hidden.append(
-                    jnp.dot(
-                        first_ref[offset : offset + count],
-                        jnp.concatenate(taps, axis=1),
-                        preferred_element_type=F32,
-                    )
+
+    def layers(device):
+        base = device * rows
+        hidden = []
+        offset = 0
+        for number, (_, _, size) in enumerate(parts):
+            taps = []
+            for side in range(rows):
+                pieces = [tile_ref[base + side + c, number] for c in range(3)]
+                pieces += [tile_ref[base + side + c, number, :again] for c in range(3)]
+                taps.append(jnp.concatenate(pieces, axis=0))
+            count = size * first_ref.shape[0] // (local + 2)
+            hidden.append(
+                jnp.dot(
+                    first_ref[offset : offset + count],
+                    jnp.concatenate(taps, axis=1),
+                    preferred_element_type=F32,
                 )
-                offset += count
-            halves = [split(jnp.maximum(piece, 0.0)) for piece in hidden]
-            pair = jnp.concatenate(
-                [high for high, _ in halves] + [low for _, low in halves], axis=0
             )
-            partial = jnp.dot(second_ref[...], pair, preferred_element_type=F32)
-            partial = partial[:partial_rows] + partial[partial_rows:]
-            for side in range(sides):
-                partial_ref[base + side + 1] = partial[:, side * columns : (side + 1) * columns]
-        return carry
-
-    lax.fori_loop(0, grid_rows // (sides * unroll), layers, 0)
+            offset += count
+        halves = [split(jnp.maximum(piece, 0.0)) for piece in hidden]
+        pair = jnp.concatenate([high for high, _ in halves] + [low for _, low in halves], axis=0)
+        partial = jnp.dot(second_ref[...], pair, preferred_element_type=F32)
+        partial = partial[:partial_rows] + partial[partial_rows:]
+        for side in range(rows):
+            partial_ref[base + side + 1] = partial[:, side * columns : (side + 1) * columns]
 
     def gather(device, most):
         for row in range(rows):
@@ -252,7 +296,25 @@
             most = jnp.maximum(most, total)
         return most
 
-    most = lax.fori_loop(0, devices, gather, zero, unroll=2)
+    def present(device):
+        return jnp.where(device < devices, 1.0, 0.0).astype(F32)
+
+    build(0, 1.0)
+    build(1, 1.0)
+    layers(0)
+    build(2, present(2))
+    layers(1)
+    build(3, present(3))
+
+    def step(device, most):
+        most = gather(device - 2, most)
+        build(device + 2, present(device + 2))
+        layers(device)
+        return most
+
+    most = lax.fori_loop(2, devices, step, zero, unroll=2)
+    most = gather(devices - 2, most)
+    most = gather(devices - 1, most)
     scale = jnp.broadcast_to(
         1.0 / (jnp.max(most, axis=1, keepdims=True) + EPSILON), most.shape
     )
@@ -286,12 +348,11 @@
 
 
 VMEM = pl.BlockSpec(memory_space=pltpu.VMEM)
-SMEM = pl.BlockSpec(memory_space=pltpu.SMEM)
+ANY = pl.BlockSpec(memory_space=pltpu.HBM)
 
 
 def shards(source_features, target_features, conv_first, conv_second):
     devices = lax.axis_size("tgt")
-    position = lax.axis_index("tgt")
     rows, columns, channels = target_features.shape
     cells = source_features.shape[0] * devices
     hid = conv_first.shape[0]
@@ -304,53 +365,71 @@
     depth = hidden * 2 * hid
     assert local <= SUBLANES and rows * devices % 4 == 0
 
-    spread = jnp.broadcast_to(source_features[None], (devices,) + source_features.shape)
-    sources = exchange(spread).reshape(cells, channels)
-
-    direct = conv_first[:, 1].reshape(hid, TAPS)
-    turned = jnp.transpose(conv_first[:, :, :, 1, :], (0, 3, 1, 2)).reshape(hid, TAPS)
-    first_taps = jnp.pad(jnp.concatenate([direct, turned]), ((0, 0), (0, TAP_PAD - TAPS)))
-    direct = conv_second[:, 1].reshape(hid, TAPS)
-    turned = jnp.transpose(conv_second[:, :, :, 1, :], (0, 3, 1, 2)).reshape(hid, TAPS)
-    second_taps = jnp.pad(jnp.concatenate([direct, turned]), ((0, 0), (0, TAP_PAD - TAPS)))
-    second_taps = jnp.tile(second_taps.T, (1, hidden))
-    edges = jnp.stack([position > 0, position < devices - 1]).astype(F32)
+    pick = jnp.asarray(first_selector(parts), BF16)
+    scatter = jnp.asarray(second_selector(local), BF16)
+    spread, target_features, pick, scatter = pl.pallas_call(
+        spread_kernel,
+        out_shape=(
+            jax.ShapeDtypeStruct((devices, source_features.shape[0], channels // 2), BF16),
+            jax.ShapeDtypeStruct(target_features.shape, BF16),
+            jax.ShapeDtypeStruct(pick.shape, BF16),
+            jax.ShapeDtypeStruct(scatter.shape, BF16),
+        ),
+        in_specs=[ANY] * 4,
+        out_specs=(VMEM,) * 4,
+        scratch_shapes=[
+            pltpu.VMEM(source_features.shape, BF16),
+            pltpu.SemaphoreType.DMA((4,)),
+        ],
+        compiler_params=room(),
+        name="spread",
+    )(
+        *(
+            pltpu.with_memory_space_constraint(value, pltpu.HBM)
+            for value in (source_features, target_features, pick, scatter)
+        )
+    )
+    mine = exchange(spread).reshape(cells, channels // 2)
+    other = lax.ppermute(mine, "tgt", [(i, i ^ 1) for i in range(devices)])
+
     second_rows = 18 * SUBLANES
     target_unit, first_weights, second_weights = pl.pallas_call(
-        functools.partial(prepare_kernel, hid),
+        functools.partial(prepare_kernel, devices),
         out_shape=(
             jax.ShapeDtypeStruct((rows * columns, channels), BF16),
             jax.ShapeDtypeStruct((depth, width), BF16),
             jax.ShapeDtypeStruct((2 * second_rows, 2 * depth), BF16),
         ),
-        in_specs=[SMEM] + [VMEM] * 5,
+        in_specs=[VMEM] * 5 + [pl.BlockSpec(memory_space=pl.ANY)],
         out_specs=(VMEM,) * 3,
+        scratch_shapes=[pltpu.VMEM((4 * TAP_PAD, 128), F32)],
         cost_estimate=pl.CostEstimate(flops=10**6, bytes_accessed=2 * 10**6, transcendentals=0),
         compiler_params=room(),
         name="prepare",
     )(
-        edges,
         target_features,
-        first_taps,
-        second_taps,
-        jnp.asarray(first_selector(parts), BF16),
-        jnp.asarray(second_selector(local), BF16),
+        jnp.transpose(conv_first, (1, 2, 3, 4, 0)),
+        jnp.transpose(conv_second, (1, 2, 3, 4, 0)),
+        pick,
+        scatter,
+        mine,
     )
 
     slots = pl.pallas_call(
         functools.partial(match_kernel, local),
         out_shape=jax.ShapeDtypeStruct((devices, rows * window + rows, columns), F32),
-        in_specs=[VMEM] * 2,
+        in_specs=[VMEM] * 3,
         out_specs=VMEM,
         scratch_shapes=[
+            pltpu.VMEM((cells, channels), BF16),
             pltpu.VMEM((rows, cells + 2 * SUBLANES, columns), F32),
         ],
         compiler_params=room(),
         name="match",
-    )(sources, target_unit)
+    )(mine, other, target_unit)
 
     stores = (
-        ((rows * devices + 2, len(parts), tile, columns), BF16),
+        ((rows * (devices + 2) + 2, len(parts), tile, columns), BF16),
         ((rows * devices + 2, second_rows, columns), F32),
     )
     slots = pl.pallas_call(

time: 51.4 us -> 49.2 us (0.957)
  blocking collectives: 24.3 us -> 39.5 us
  starting transfers between devices: 7.55 us -> 0.01 us
  waiting for transfers between devices: 6.83 us -> 0.66 us
  local copies, waits for them, and re-layouts: 3.2 us -> 0.01 us
    all_to_all x2 -> x3, blocking collectives: 24.3 us -> 39.5 us  [exchange(): return lax.all_to_all(slots, 'tgt', 0, 0, tiled=True)]
    all_to_all x1 -> x0, starting transfers between devices: 7.55 us -> none  [exchange(): return lax.all_to_all(slots, 'tgt', 0, 0, tiled=True)]
    all_to_all x1 -> x0, waiting for transfers between devices: 6.83 us -> none  [exchange(): return lax.all_to_all(slots, 'tgt', 0, 0, tiled=True)]
    broadcast_in_dim x1 -> x0, local copies, waits for them, and re-layouts: 1.45 us -> none  [shards(): jnp.broadcast_to(source_features[None], (devices,) + source_features.shape)]
    pallas_call x1, Pallas kernels: 6.48 us -> 5.55 us  [shards(): pl.pallas_call(functools.partial(consensus_kernel, parts, local, rows), o...]
    unnamed x10 -> x4, local copies, waits for them, and re-layouts: 0.83 us -> 0.01 us
    pallas_call x1 -> x2, Pallas kernels: 1.16 us -> 1.89 us  [the longest x1 1.22 us: shards(): pl.pallas_call(spread_kernel, out_shape=(jax.ShapeDtypeStruct((devices, s...]
    ppermute x0 -> x1, waiting for transfers between devices: none -> 0.66 us  [shards(): other = lax.ppermute(mine, 'tgt', [(i, i ^ 1) for i in range(devices)])]
  transfers between devices with their start and end apart: 1 -> 1, of which waited for: 1 -> 1; matrix products, arithmetic and copies ran while one was open for 1% -> 0% of each run, Pallas kernels for 2% -> 1%
where the time goes in v1:
time: 49.2 us; the launch traced here: 48.9 us
  blocking collectives  39.5 us (80%)
  Pallas kernels  8.64 us (18%)
  waiting for transfers between devices  0.66 us (1%)
    all_to_all x3, blocking collectives, exchange(): return lax.all_to_all(slots, 'tgt', 0, 0, tiled=True)  39.5 us
    pallas_call x1, Pallas kernels, shards(): pl.pallas_call(functools.partial(consensus_kernel, parts, local, rows), o...  5.55 us
    pallas_call x1, Pallas kernels, shards(): pl.pallas_call(spread_kernel, out_shape=(jax.ShapeDtypeStruct((devices, s...  1.22 us
  transfers between devices with their start and end apart: 1, of which 1 were waited for; matrix products, arithmetic and copies ran while one was open for 0% of the time, Pallas kernels for 1%

profile of v1, /device:TPU:0, one launch (start us, length us, event | category | flops | bytes accessed | tf_op | source)
XLA Modules:
  0.0 48.9 jit_solution(9614393265464074360)
XLA Ops:
  0.0 1.2 %spread.1 = (bf16[16,8,512]{2,1,0:T(8,128)(2,1)S(1)}, bf16[2,128,1024]{2,1,0:T(8,128)(2,1)S(1)}, bf16[64,2400]{1,0:T(8,128)(2,1)S(1)}, bf16[144,640]{1,0:T(8,128)(2,1)S(1)}) custom-call(bf16[8,1024]{1,0:T(8,128)(2,1)} %source_ref.1, bf16[2,128,1024]{2,1,0:T(8,128)(2,1)} %target_ref.1, bf16[64,2400]{1,0:T(8,128)(2,1)} %constant.4.clone.pick_ref, ...), custom_call_target="tpu_custom_call" | custom-call | tf_op jit(solution)/shard_map/spread/pallas_call | solution.py:370
  1.2 0.0 copy-start
  1.2 0.0 copy-start.1
  1.3 15.2 %all_to_all.15 = bf16[16,8,512]{2,1,0:T(8,128)(2,1)S(1)} all-to-all(bf16[16,8,512]{2,1,0:T(8,128)(2,1)S(1)} %get-tuple-element.12), channel_id=1, replica_groups=mesh['pairs'=2,'tgt'=16] {'tgt'}, dimensions={0} | all-to-all | bytes 262144 | tf_op jit(solution)/shard_map/all_to_all | solution.py:342
  16.5 0.0 collective-permute-start
  16.5 0.0 copy-done
  16.5 0.0 copy-done.1
  16.5 0.7 %prepare.1 = (bf16[256,1024]{1,0:T(8,128)(2,1)S(1)}, bf16[320,240]{1,0:T(8,128)(2,1)S(1)}, bf16[288,640]{1,0:T(8,128)(2,1)S(1)}) custom-call(bf16[2,128,1024]{2,1,0:T(8,128)(2,1)S(1)} %get-tuple-element.13.target_ref, f32[3,3,3,3,16]{4,3,2,1,0:T(4,128)S(1)} %bitcast.7, f32[3,3,3,3,16]{4,3,2,1,0:T(4,128)S(1)} %bitcast.8, ...), custom_call_target="tpu_custom_call" | custom-call | flops 1000000 | bytes 2000000 | tf_op jit(solution)/shard_map/prepare/pallas_call | solution.py:396
  17.2 0.7 %collective-permute-done.other_ref = bf16[128,512]{1,0:T(8,128)(2,1)S(1)} collective-permute-done((bf16[128,512]{1,0:T(8,128)(2,1)S(1)}, bf16[128,512]{1,0:T(8,128)(2,1)S(1)}, u32[]{:S(2)}, u32[]{:S(2)}) %collective-permute-start) | collective-permute-done | bytes 131104 | tf_op jit(solution)/shard_map/ppermute | solution.py:393
  17.9 0.4 match.1
  18.3 12.6 %all_to_all.16.came_ref = f32[16,26,128]{2,1,0:T(8,128)S(1)} all-to-all(f32[16,26,128]{2,1,0:T(8,128)S(1)} %match.1), channel_id=1, replica_groups=mesh['pairs'=2,'tgt'=16] {'tgt'}, dimensions={0} | all-to-all | bytes 425984 | tf_op jit(solution)/shard_map/all_to_all | solution.py:342
  30.9 5.6 %consensus.1 = f32[16,24,128]{2,1,0:T(8,128)S(1)} custom-call(f32[16,26,128]{2,1,0:T(8,128)S(1)} %all_to_all.16.came_ref, bf16[320,240]{1,0:T(8,128)(2,1)S(1)} %get-tuple-element.17.first_ref, bf16[288,640]{1,0:T(8,128)(2,1)S(1)} %get-tuple-element.18.second_ref), custom_call_target="tpu_custom_call" | custom-call | tf_op jit(solution)/shard_map/consensus/pallas_call | solution.py:435
  36.5 11.7 %all_to_all.17.came_ref = f32[16,24,128]{2,1,0:T(8,128)S(1)} all-to-all(f32[16,24,128]{2,1,0:T(8,128)S(1)} %consensus.1), channel_id=1, replica_groups=mesh['pairs'=2,'tgt'=16] {'tgt'}, dimensions={0} | all-to-all | bytes 393216 | tf_op jit(solution)/shard_map/all_to_all | solution.py:342
  48.1 0.8 %finish.1 = f32[128,2,128]{2,1,0:T(2,128)} custom-call(f32[16,24,128]{2,1,0:T(8,128)S(1)} %all_to_all.17.came_ref), custom_call_target="tpu_custom_call" | custom-call | tf_op jit(solution)/shard_map/finish/pallas_call | solution.py:445
Async XLA Ops:
  1.2 15.3 %copy-start = (f32[16,3,3,3,3]{0,4,3,2,1:T(4,128)S(1)}, f32[16,3,3,3,3]{0,4,3,2,1:T(4,128)}, u32[]{:S(2)}) copy-start(f32[16,3,3,3,3]{0,4,3,2,1:T(4,128)} %param.8) | copy-start | bytes 15556
  1.2 15.3 %copy-start.1 = (f32[16,3,3,3,3]{0,4,3,2,1:T(4,128)S(1)}, f32[16,3,3,3,3]{0,4,3,2,1:T(4,128)}, u32[]{:S(2)}) copy-start(f32[16,3,3,3,3]{0,4,3,2,1:T(4,128)} %param.9) | copy-start | bytes 15556
  16.5 1.3 %collective-permute-start = (bf16[128,512]{1,0:T(8,128)(2,1)S(1)}, bf16[128,512]{1,0:T(8,128)(2,1)S(1)}, u32[]{:S(2)}, u32[]{:S(2)}) collective-permute-start(bf16[128,512]{1,0:T(8,128)(2,1)S(1)} %bitcast.4), channel_id=1, source_target_pairs={{0,1},{1,0},{2,3},{3,2},{4,5},{5,4},{6,7},{7,6},{8,9},{9,8},{10,11... | collective-permute-start | bytes 393224 | tf_op jit(solution)/shard_map/ppermute | solution.py:393

commit v2 on v1

--- a/solution.py
+++ b/solution.py
@@ -183,11 +183,23 @@
         inverse = 1.0 / (source_best + EPSILON)
         for target in range(send_ref.shape[0]):
             first = SUBLANES + target * local - 2
-            send_ref[target, row * window : (row + 1) * window] = order_ref[
+            send_ref[target, row * window : (row + 1) * window, 0, :] = order_ref[
                 row, first : first + window, :
             ]
             place = rows * window + row
-            send_ref[target, place : place + 1] = inverse
+            send_ref[target, place : place + 1, 0, :] = inverse
+
+
+def row_of_column(column, lanes):
+    row = lax.broadcasted_iota(jnp.int32, (column.shape[0], lanes), 0)
+    lane = lax.broadcasted_iota(jnp.int32, (column.shape[0], lanes), 1)
+    return jnp.sum(jnp.where(row == lane, column, 0.0), axis=0, keepdims=True)
+
+
+def column_of_row(values, count):
+    row = lax.broadcasted_iota(jnp.int32, (count, values.shape[1]), 0)
+    lane = lax.broadcasted_iota(jnp.int32, (count, values.shape[1]), 1)
+    return jnp.sum(jnp.where(row == lane, values, 0.0), axis=1, keepdims=True)
 
 
 def lane_shifts(value):
@@ -200,9 +212,9 @@
 
 
 def consensus_kernel(
-    parts, local, rows, came_ref, first_ref, second_ref, send_ref, tile_ref, partial_ref
+    parts, local, rows, came_ref, first_ref, second_ref, send_ref, tile_ref, partial_ref, rows_ref
 ):
-    devices, _, columns = came_ref.shape
+    devices, columns = came_ref.shape[0], came_ref.shape[3]
     window = max(SUBLANES, local + 4)
     grid_rows = devices * rows
     tile = len(ORDER) * SUBLANES
@@ -210,13 +222,15 @@
     zero = jnp.zeros((SUBLANES, columns), F32)
 
     def piece_of(device, row, first):
-        return came_ref[device, row * window + first : row * window + first + SUBLANES, :]
+        return rows_ref[device * rows + row, first : first + SUBLANES, :]
 
     def survey(device, best):
         best = list(best)
-        for number, (first, _, _) in enumerate(parts):
-            for row in range(rows):
-                best[number] = jnp.maximum(best[number], piece_of(device, row, first))
+        for row in range(rows):
+            block = came_ref[device, row * window : (row + 1) * window, 0, :]
+            rows_ref[device * rows + row, :window] = block
+            for number, (first, _, _) in enumerate(parts):
+                best[number] = jnp.maximum(best[number], block[first : first + SUBLANES])
         return tuple(best)
 
     best = lax.fori_loop(0, devices, survey, (zero,) * len(parts), unroll=4)
@@ -233,7 +247,7 @@
         source = jnp.minimum(device, devices - 1)
         for row in range(rows):
             place = rows * window + row
-            inverse = came_ref[source, place : place + 1, :] * present
+            inverse = came_ref[source, place : place + 1, 0, :] * present
             for number, (first, _, _) in enumerate(parts):
                 value = piece_of(source, row, first)
                 value = value * (value * inverse) * (value * scales[number])
@@ -292,7 +306,7 @@
                 output = lane_shifts(sums[0])[0] + sums[1] + lane_shifts(sums[2])[1]
                 output = jnp.maximum(output, 0.0)
                 total = output if total is None else total + output
-            send_ref[device, row * SUBLANES : (row + 1) * SUBLANES] = total
+            send_ref[device, row * SUBLANES : (row + 1) * SUBLANES, 0, :] = total
             most = jnp.maximum(most, total)
         return most
 
@@ -315,26 +329,29 @@
     most = lax.fori_loop(2, devices, step, zero, unroll=2)
     most = gather(devices - 2, most)
     most = gather(devices - 1, most)
-    scale = jnp.broadcast_to(
-        1.0 / (jnp.max(most, axis=1, keepdims=True) + EPSILON), most.shape
-    )
+    best = jnp.max(most, axis=1, keepdims=True)
+    scale = row_of_column(1.0 / (best + EPSILON), columns)
     for device in range(devices):
-        send_ref[device, rows * SUBLANES :] = scale
+        send_ref[device, rows * SUBLANES : rows * SUBLANES + 1, 0, :] = scale
 
 
 def finish_kernel(local, came_ref, out_ref):
     devices = came_ref.shape[0]
     rows = out_ref.shape[1]
+    place = rows * SUBLANES
+    scales = [
+        column_of_row(came_ref[device, place : place + 1, 0, :], SUBLANES)
+        for device in range(devices)
+    ]
     for row in range(rows):
         first = row * SUBLANES
-        most = came_ref[0, first : first + SUBLANES]
+        most = came_ref[0, first : first + SUBLANES, 0, :]
         for device in range(1, devices):
-            most = jnp.maximum(most, came_ref[device, first : first + SUBLANES])
+            most = jnp.maximum(most, came_ref[device, first : first + SUBLANES, 0, :])
         inverse = 1.0 / (jnp.max(most, axis=0, keepdims=True) + EPSILON)
         for device in range(devices):
-            value = came_ref[device, first : first + SUBLANES]
-            scale = came_ref[device, rows * SUBLANES :]
-            value = value * (value * inverse) * (value * scale)
+            value = came_ref[device, first : first + SUBLANES, 0, :]
+            value = value * (value * inverse) * (value * scales[device])
             out_ref[device * local : (device + 1) * local, row, :] = value[:local]
 
 
@@ -417,7 +434,7 @@
 
     slots = pl.pallas_call(
         functools.partial(match_kernel, local),
-        out_shape=jax.ShapeDtypeStruct((devices, rows * window + rows, columns), F32),
+        out_shape=jax.ShapeDtypeStruct((devices, rows * window + rows, 1, columns), F32),
         in_specs=[VMEM] * 3,
         out_specs=VMEM,
         scratch_shapes=[
@@ -431,10 +448,11 @@
     stores = (
         ((rows * (devices + 2) + 2, len(parts), tile, columns), BF16),
         ((rows * devices + 2, second_rows, columns), F32),
+        ((rows * devices, -(-window // SUBLANES) * SUBLANES, columns), F32),
     )
     slots = pl.pallas_call(
         functools.partial(consensus_kernel, parts, local, rows),
-        out_shape=jax.ShapeDtypeStruct((devices, (rows + 1) * SUBLANES, columns), F32),
+        out_shape=jax.ShapeDtypeStruct((devices, rows * SUBLANES + 1, 1, columns), F32),
         in_specs=[VMEM] * 3,
         out_specs=VMEM,
         scratch_shapes=[pltpu.VMEM(shape, kind) for shape, kind in stores],

time: 49.2 us -> 47.7 us (0.970)
  blocking collectives: 39.5 us -> 37.7 us
    all_to_all x3, blocking collectives: 39.5 us -> 37.7 us  [exchange(): return lax.all_to_all(slots, 'tgt', 0, 0, tiled=True)]
where the time goes in v2:
time: 47.7 us; the launch traced here: 47.4 us
  blocking collectives  37.7 us (79%)
  Pallas kernels  8.97 us (19%)
  waiting for transfers between devices  0.66 us (1%)
    all_to_all x3, blocking collectives, exchange(): return lax.all_to_all(slots, 'tgt', 0, 0, tiled=True)  37.7 us
    pallas_call x1, Pallas kernels, shards(): pl.pallas_call(functools.partial(consensus_kernel, parts, local, rows), o...  5.72 us
    pallas_call x1, Pallas kernels, shards(): pl.pallas_call(spread_kernel, out_shape=(jax.ShapeDtypeStruct((devices, s...  1.22 us
  transfers between devices with their start and end apart: 1, of which 1 were waited for; matrix products, arithmetic and copies ran while one was open for 0% of the time, Pallas kernels for 1%

profile of v2, /device:TPU:0, one launch (start us, length us, event | category | flops | bytes accessed | tf_op | source)
XLA Modules:
  0.0 47.4 jit_solution(483420957819186064)
XLA Ops:
  0.0 1.2 %spread.1 = (bf16[16,8,512]{2,1,0:T(8,128)(2,1)S(1)}, bf16[2,128,1024]{2,1,0:T(8,128)(2,1)S(1)}, bf16[64,2400]{1,0:T(8,128)(2,1)S(1)}, bf16[144,640]{1,0:T(8,128)(2,1)S(1)}) custom-call(bf16[8,1024]{1,0:T(8,128)(2,1)} %source_ref.1, bf16[2,128,1024]{2,1,0:T(8,128)(2,1)} %target_ref.1, bf16[64,2400]{1,0:T(8,128)(2,1)} %constant.4.clone.pick_ref, ...), custom_call_target="tpu_custom_call" | custom-call | tf_op jit(solution)/shard_map/spread/pallas_call | solution.py:387
  1.2 0.0 copy-start
  1.2 0.0 copy-start.1
  1.3 15.2 %all_to_all.15 = bf16[16,8,512]{2,1,0:T(8,128)(2,1)S(1)} all-to-all(bf16[16,8,512]{2,1,0:T(8,128)(2,1)S(1)} %get-tuple-element.12), channel_id=1, replica_groups=mesh['pairs'=2,'tgt'=16] {'tgt'}, dimensions={0} | all-to-all | bytes 262144 | tf_op jit(solution)/shard_map/all_to_all | solution.py:359
  16.5 0.0 collective-permute-start
  16.5 0.0 copy-done
  16.5 0.0 copy-done.1
  16.5 0.7 %prepare.1 = (bf16[256,1024]{1,0:T(8,128)(2,1)S(1)}, bf16[320,240]{1,0:T(8,128)(2,1)S(1)}, bf16[288,640]{1,0:T(8,128)(2,1)S(1)}) custom-call(bf16[2,128,1024]{2,1,0:T(8,128)(2,1)S(1)} %get-tuple-element.13.target_ref, f32[3,3,3,3,16]{4,3,2,1,0:T(4,128)S(1)} %bitcast.7, f32[3,3,3,3,16]{4,3,2,1,0:T(4,128)S(1)} %bitcast.8, ...), custom_call_target="tpu_custom_call" | custom-call | flops 1000000 | bytes 2000000 | tf_op jit(solution)/shard_map/prepare/pallas_call | solution.py:413
  17.2 0.7 %collective-permute-done.other_ref = bf16[128,512]{1,0:T(8,128)(2,1)S(1)} collective-permute-done((bf16[128,512]{1,0:T(8,128)(2,1)S(1)}, bf16[128,512]{1,0:T(8,128)(2,1)S(1)}, u32[]{:S(2)}, u32[]{:S(2)}) %collective-permute-start) | collective-permute-done | bytes 131104 | tf_op jit(solution)/shard_map/ppermute | solution.py:410
  17.9 0.5 %match.1 = f32[16,26,1,128]{3,2,1,0:T(1,128)S(1)} custom-call(bf16[128,512]{1,0:T(8,128)(2,1)S(1)} %bitcast.6, bf16[128,512]{1,0:T(8,128)(2,1)S(1)} %collective-permute-done.other_ref, bf16[256,1024]{1,0:T(8,128)(2,1)S(1)} %get-tuple-element.16.target_ref), custom_call_target="tpu_custom_call" | custom-call | tf_op jit(solution)/shard_map/match/pallas_call | solution.py:435
  18.4 11.8 %all_to_all.16.came_ref = f32[16,26,1,128]{3,2,1,0:T(1,128)S(1)} all-to-all(f32[16,26,1,128]{3,2,1,0:T(1,128)S(1)} %match.1), channel_id=1, replica_groups=mesh['pairs'=2,'tgt'=16] {'tgt'}, dimensions={0} | all-to-all | bytes 425984 | tf_op jit(solution)/shard_map/all_to_all | solution.py:359
  30.2 5.7 %consensus.1 = f32[16,17,1,128]{3,2,1,0:T(1,128)S(1)} custom-call(f32[16,26,1,128]{3,2,1,0:T(1,128)S(1)} %all_to_all.16.came_ref, bf16[320,240]{1,0:T(8,128)(2,1)S(1)} %get-tuple-element.17.first_ref, bf16[288,640]{1,0:T(8,128)(2,1)S(1)} %get-tuple-element.18.second_ref), custom_call_target="tpu_custom_call" | custom-call | tf_op jit(solution)/shard_map/consensus/pallas_call | solution.py:453
  35.9 10.6 %all_to_all.17.came_ref = f32[16,17,1,128]{3,2,1,0:T(1,128)S(1)} all-to-all(f32[16,17,1,128]{3,2,1,0:T(1,128)S(1)} %consensus.1), channel_id=1, replica_groups=mesh['pairs'=2,'tgt'=16] {'tgt'}, dimensions={0} | all-to-all | bytes 278528 | tf_op jit(solution)/shard_map/all_to_all | solution.py:359
  46.5 0.8 %finish.1 = f32[128,2,128]{2,1,0:T(2,128)} custom-call(f32[16,17,1,128]{3,2,1,0:T(1,128)S(1)} %all_to_all.17.came_ref), custom_call_target="tpu_custom_call" | custom-call | tf_op jit(solution)/shard_map/finish/pallas_call | solution.py:463
Async XLA Ops:
  1.2 15.3 %copy-start = (f32[16,3,3,3,3]{0,4,3,2,1:T(4,128)S(1)}, f32[16,3,3,3,3]{0,4,3,2,1:T(4,128)}, u32[]{:S(2)}) copy-start(f32[16,3,3,3,3]{0,4,3,2,1:T(4,128)} %param.8) | copy-start | bytes 15556
  1.2 15.3 %copy-start.1 = (f32[16,3,3,3,3]{0,4,3,2,1:T(4,128)S(1)}, f32[16,3,3,3,3]{0,4,3,2,1:T(4,128)}, u32[]{:S(2)}) copy-start(f32[16,3,3,3,3]{0,4,3,2,1:T(4,128)} %param.9) | copy-start | bytes 15556
  16.5 1.3 %collective-permute-start = (bf16[128,512]{1,0:T(8,128)(2,1)S(1)}, bf16[128,512]{1,0:T(8,128)(2,1)S(1)}, u32[]{:S(2)}, u32[]{:S(2)}) collective-permute-start(bf16[128,512]{1,0:T(8,128)(2,1)S(1)} %bitcast.4), channel_id=1, source_target_pairs={{0,1},{1,0},{2,3},{3,2},{4,5},{5,4},{6,7},{7,6},{8,9},{9,8},{10,11... | collective-permute-start | bytes 393224 | tf_op jit(solution)/shard_map/ppermute | solution.py:410

commit v3 on v2

--- a/solution.py
+++ b/solution.py
@@ -9,12 +9,17 @@
 from jax.sharding import PartitionSpec as P
 
 EPSILON = 1e-05
+TINY = 1e-30
 F32 = jnp.float32
 BF16 = jnp.bfloat16
 TAP_PAD = 32
 SUBLANES = 8
 ORDER = ((0, 0), (1, 0), (2, 0), (0, 1), (1, 1), (2, 1))
 REPEATED = 4
+
+
+def whole_tiles(count):
+    return -(-count // SUBLANES) * SUBLANES
 
 
 def parts_of(local):
@@ -180,14 +185,33 @@
             :, row * columns : (row + 1) * columns
         ]
         source_best = jnp.max(order_ref[row], axis=0, keepdims=True)
-        inverse = 1.0 / (source_best + EPSILON)
+        scale = 1.0 / jnp.maximum(source_best, TINY)
+        root = jnp.concatenate(root_rows(source_best), axis=0)
+        place = rows * window + 2 * row
         for target in range(send_ref.shape[0]):
             first = SUBLANES + target * local - 2
-            send_ref[target, row * window : (row + 1) * window, 0, :] = order_ref[
-                row, first : first + window, :
-            ]
-            place = rows * window + row
-            send_ref[target, place : place + 1, 0, :] = inverse
+            send_ref[target, row * window : (row + 1) * window] = (
+                order_ref[row, first : first + window, :] * scale
+            )
+            send_ref[target, place : place + 2] = root
+    used = rows * (window + 2)
+    spare = send_ref.shape[1] - used
+    if spare:
+        for target in range(send_ref.shape[0]):
+            send_ref[target, used:] = jnp.zeros((spare, columns), F32)
+
+
+def root_rows(best):
+    root = jnp.sqrt(jnp.sqrt(jnp.sqrt(best)))
+    high = root.astype(BF16).astype(F32)
+    return high, root - high
+
+
+def best_of_root(rows):
+    root = rows[:1] + rows[1:]
+    for _ in range(3):
+        root = root * root
+    return root
 
 
 def row_of_column(column, lanes):
@@ -214,7 +238,7 @@
 def consensus_kernel(
     parts, local, rows, came_ref, first_ref, second_ref, send_ref, tile_ref, partial_ref, rows_ref
 ):
-    devices, columns = came_ref.shape[0], came_ref.shape[3]
+    devices, _, columns = came_ref.shape
     window = max(SUBLANES, local + 4)
     grid_rows = devices * rows
     tile = len(ORDER) * SUBLANES
@@ -227,8 +251,11 @@
     def survey(device, best):
         best = list(best)
         for row in range(rows):
-            block = came_ref[device, row * window : (row + 1) * window, 0, :]
+            place = rows * window + 2 * row
+            largest = best_of_root(came_ref[device, place : place + 2])
+            block = came_ref[device, row * window : (row + 1) * window] * largest
             rows_ref[device * rows + row, :window] = block
+            rows_ref[device * rows + row, window : window + 1] = 1.0 / (largest + EPSILON)
             for number, (first, _, _) in enumerate(parts):
                 best[number] = jnp.maximum(best[number], block[first : first + SUBLANES])
         return tuple(best)
@@ -246,8 +273,7 @@
     def build(device, present):
         source = jnp.minimum(device, devices - 1)
         for row in range(rows):
-            place = rows * window + row
-            inverse = came_ref[source, place : place + 1, 0, :] * present
+            inverse = rows_ref[source * rows + row, window : window + 1, :] * present
             for number, (first, _, _) in enumerate(parts):
                 value = piece_of(source, row, first)
                 value = value * (value * inverse) * (value * scales[number])
@@ -306,7 +332,7 @@
                 output = lane_shifts(sums[0])[0] + sums[1] + lane_shifts(sums[2])[1]
                 output = jnp.maximum(output, 0.0)
                 total = output if total is None else total + output
-            send_ref[device, row * SUBLANES : (row + 1) * SUBLANES, 0, :] = total
+            send_ref[device, row * SUBLANES : (row + 1) * SUBLANES] = total
             most = jnp.maximum(most, total)
         return most
 
@@ -330,33 +356,47 @@
     most = gather(devices - 2, most)
     most = gather(devices - 1, most)
     best = jnp.max(most, axis=1, keepdims=True)
-    scale = row_of_column(1.0 / (best + EPSILON), columns)
+    scale = 1.0 / jnp.maximum(best, TINY)
+    root = jnp.concatenate(
+        [row_of_column(piece, columns) for piece in root_rows(best)]
+        + [jnp.zeros((SUBLANES - 2, columns), F32)],
+        axis=0,
+    )
     for device in range(devices):
-        send_ref[device, rows * SUBLANES : rows * SUBLANES + 1, 0, :] = scale
+        for row in range(rows):
+            start = row * SUBLANES
+            send_ref[device, start : start + SUBLANES] = (
+                send_ref[device, start : start + SUBLANES] * scale
+            )
+        send_ref[device, rows * SUBLANES :] = root
 
 
 def finish_kernel(local, came_ref, out_ref):
-    devices = came_ref.shape[0]
+    devices, _, columns = came_ref.shape
     rows = out_ref.shape[1]
     place = rows * SUBLANES
-    scales = [
-        column_of_row(came_ref[device, place : place + 1, 0, :], SUBLANES)
+    bests = [
+        column_of_row(best_of_root(came_ref[device, place : place + 2]), SUBLANES)
         for device in range(devices)
     ]
     for row in range(rows):
         first = row * SUBLANES
-        most = came_ref[0, first : first + SUBLANES, 0, :]
-        for device in range(1, devices):
-            most = jnp.maximum(most, came_ref[device, first : first + SUBLANES, 0, :])
+        most = jnp.zeros((SUBLANES, columns), F32)
+        for device in range(devices):
+            most = jnp.maximum(most, came_ref[device, first : first + SUBLANES] * bests[device])
         inverse = 1.0 / (jnp.max(most, axis=0, keepdims=True) + EPSILON)
         for device in range(devices):
-            value = came_ref[device, first : first + SUBLANES, 0, :]
-            value = value * (value * inverse) * (value * scales[device])
+            value = came_ref[device, first : first + SUBLANES] * bests[device]
+            value = value * (value * inverse) * (value * (1.0 / (bests[device] + EPSILON)))
             out_ref[device * local : (device + 1) * local, row, :] = value[:local]
 
 
 def exchange(slots):
     return lax.all_to_all(slots, "tgt", 0, 0, tiled=True)
+
+
+def exchange_relative(slots):
+    return exchange(slots.astype(jnp.float16)).astype(F32)
 
 
 def room(*shapes):
@@ -434,7 +474,7 @@
 
     slots = pl.pallas_call(
         functools.partial(match_kernel, local),
-        out_shape=jax.ShapeDtypeStruct((devices, rows * window + rows, 1, columns), F32),
+        out_shape=jax.ShapeDtypeStruct((devices, whole_tiles(rows * (window + 2)), columns), F32),
         in_specs=[VMEM] * 3,
         out_specs=VMEM,
         scratch_shapes=[
@@ -448,17 +488,17 @@
     stores = (
         ((rows * (devices + 2) + 2, len(parts), tile, columns), BF16),
         ((rows * devices + 2, second_rows, columns), F32),
-        ((rows * devices, -(-window // SUBLANES) * SUBLANES, columns), F32),
+        ((rows * devices, whole_tiles(window + 1), columns), F32),
     )
     slots = pl.pallas_call(
         functools.partial(consensus_kernel, parts, local, rows),
-        out_shape=jax.ShapeDtypeStruct((devices, rows * SUBLANES + 1, 1, columns), F32),
+        out_shape=jax.ShapeDtypeStruct((devices, (rows + 1) * SUBLANES, columns), F32),
         in_specs=[VMEM] * 3,
         out_specs=VMEM,
         scratch_shapes=[pltpu.VMEM(shape, kind) for shape, kind in stores],
         compiler_params=room(*stores),
         name="consensus",
-    )(exchange(slots), first_weights, second_weights)
+    )(exchange_relative(slots), first_weights, second_weights)
 
     filtered = pl.pallas_call(
         functools.partial(finish_kernel, local),
@@ -467,7 +507,7 @@
         out_specs=VMEM,
         compiler_params=room(),
         name="finish",
-    )(exchange(slots))
+    )(exchange_relative(slots))
     return filtered[None]
 
 

time: 47.7 us -> 45.8 us (0.960)
  blocking collectives: 37.7 us -> 35.7 us
    all_to_all x3, blocking collectives: 37.7 us -> 35.7 us  [exchange(): return lax.all_to_all(slots, 'tgt', 0, 0, tiled=True)]
where the time goes in v3:
time: 45.8 us; the launch traced here: 45.4 us
  blocking collectives  35.7 us (78%)
  Pallas kernels  8.89 us (19%)
  waiting for transfers between devices  0.66 us (1%)
    all_to_all x3, blocking collectives, exchange(): return lax.all_to_all(slots, 'tgt', 0, 0, tiled=True)  35.7 us
    pallas_call x1, Pallas kernels, shards(): pl.pallas_call(functools.partial(consensus_kernel, parts, local, rows), o...  5.68 us
    pallas_call x1, Pallas kernels, shards(): pl.pallas_call(spread_kernel, out_shape=(jax.ShapeDtypeStruct((devices, s...  1.22 us
  transfers between devices with their start and end apart: 1, of which 1 were waited for; matrix products, arithmetic and copies ran while one was open for 0% of the time, Pallas kernels for 1%

profile of v3, /device:TPU:0, one launch (start us, length us, event | category | flops | bytes accessed | tf_op | source)
XLA Modules:
  0.0 45.4 jit_solution(15987042772343088971)
XLA Ops:
  0.0 1.2 %spread.1 = (bf16[16,8,512]{2,1,0:T(8,128)(2,1)S(1)}, bf16[2,128,1024]{2,1,0:T(8,128)(2,1)S(1)}, bf16[64,2400]{1,0:T(8,128)(2,1)S(1)}, bf16[144,640]{1,0:T(8,128)(2,1)S(1)}) custom-call(bf16[8,1024]{1,0:T(8,128)(2,1)} %source_ref.1, bf16[2,128,1024]{2,1,0:T(8,128)(2,1)} %target_ref.1, bf16[64,2400]{1,0:T(8,128)(2,1)} %constant.4.clone.pick_ref, ...), custom_call_target="tpu_custom_call" | custom-call | tf_op jit(solution)/shard_map/spread/pallas_call | solution.py:427
  1.2 0.0 copy-start
  1.2 0.0 copy-start.1
  1.3 15.2 %all_to_all.15 = bf16[16,8,512]{2,1,0:T(8,128)(2,1)S(1)} all-to-all(bf16[16,8,512]{2,1,0:T(8,128)(2,1)S(1)} %get-tuple-element.12), channel_id=1, replica_groups=mesh['pairs'=2,'tgt'=16] {'tgt'}, dimensions={0} | all-to-all | bytes 262144 | tf_op jit(solution)/shard_map/all_to_all | solution.py:395
  16.5 0.0 collective-permute-start
  16.5 0.0 copy-done
  16.5 0.0 copy-done.1
  16.5 0.7 %prepare.1 = (bf16[256,1024]{1,0:T(8,128)(2,1)S(1)}, bf16[320,240]{1,0:T(8,128)(2,1)S(1)}, bf16[288,640]{1,0:T(8,128)(2,1)S(1)}) custom-call(bf16[2,128,1024]{2,1,0:T(8,128)(2,1)S(1)} %get-tuple-element.13.target_ref, f32[3,3,3,3,16]{4,3,2,1,0:T(4,128)S(1)} %bitcast.7, f32[3,3,3,3,16]{4,3,2,1,0:T(4,128)S(1)} %bitcast.8, ...), custom_call_target="tpu_custom_call" | custom-call | flops 1000000 | bytes 2000000 | tf_op jit(solution)/shard_map/prepare/pallas_call | solution.py:453
  17.2 0.7 %collective-permute-done.other_ref = bf16[128,512]{1,0:T(8,128)(2,1)S(1)} collective-permute-done((bf16[128,512]{1,0:T(8,128)(2,1)S(1)}, bf16[128,512]{1,0:T(8,128)(2,1)S(1)}, u32[]{:S(2)}, u32[]{:S(2)}) %collective-permute-start) | collective-permute-done | bytes 131104 | tf_op jit(solution)/shard_map/ppermute | solution.py:450
  17.9 0.5 %match.1 = f32[16,32,128]{2,1,0:T(8,128)S(1)} custom-call(bf16[128,512]{1,0:T(8,128)(2,1)S(1)} %bitcast.6, bf16[128,512]{1,0:T(8,128)(2,1)S(1)} %collective-permute-done.other_ref, bf16[256,1024]{1,0:T(8,128)(2,1)S(1)} %get-tuple-element.16.target_ref), custom_call_target="tpu_custom_call" | custom-call | tf_op jit(solution)/shard_map/match/pallas_call | solution.py:475
  18.4 10.5 %all_to_all.16 = f16[16,32,128]{2,1,0:T(8,128)(2,1)S(1)} all-to-all(f16[16,32,128]{2,1,0:T(8,128)(2,1)S(1)} %convert_element_type.12), channel_id=1, replica_groups=mesh['pairs'=2,'tgt'=16] {'tgt'}, dimensions={0} | all-to-all | bytes 262144 | tf_op jit(solution)/shard_map/all_to_all | solution.py:395
  28.9 5.7 %consensus.1 = f32[16,24,128]{2,1,0:T(8,128)S(1)} custom-call(f32[16,32,128]{2,1,0:T(8,128)S(1)} %convert_element_type.13.came_ref, bf16[320,240]{1,0:T(8,128)(2,1)S(1)} %get-tuple-element.17.first_ref, bf16[288,640]{1,0:T(8,128)(2,1)S(1)} %get-tuple-element.18.second_ref), custom_call_target="tpu_custom_call" | custom-call | tf_op jit(solution)/shard_map/consensus/pallas_call | solution.py:493
  34.6 10.0 %all_to_all.17 = f16[16,24,128]{2,1,0:T(8,128)(2,1)S(1)} all-to-all(f16[16,24,128]{2,1,0:T(8,128)(2,1)S(1)} %convert_element_type.14), channel_id=1, replica_groups=mesh['pairs'=2,'tgt'=16] {'tgt'}, dimensions={0} | all-to-all | bytes 196608 | tf_op jit(solution)/shard_map/all_to_all | solution.py:395
  44.6 0.9 %finish.1 = f32[128,2,128]{2,1,0:T(2,128)} custom-call(f32[16,24,128]{2,1,0:T(8,128)S(1)} %convert_element_type.15.came_ref), custom_call_target="tpu_custom_call" | custom-call | tf_op jit(solution)/shard_map/finish/pallas_call | solution.py:503
  (4 shorter events, 0.1 us)
Async XLA Ops:
  1.2 15.3 %copy-start = (f32[16,3,3,3,3]{0,4,3,2,1:T(4,128)S(1)}, f32[16,3,3,3,3]{0,4,3,2,1:T(4,128)}, u32[]{:S(2)}) copy-start(f32[16,3,3,3,3]{0,4,3,2,1:T(4,128)} %param.8) | copy-start | bytes 15556
  1.2 15.3 %copy-start.1 = (f32[16,3,3,3,3]{0,4,3,2,1:T(4,128)S(1)}, f32[16,3,3,3,3]{0,4,3,2,1:T(4,128)}, u32[]{:S(2)}) copy-start(f32[16,3,3,3,3]{0,4,3,2,1:T(4,128)} %param.9) | copy-start | bytes 15556
  16.5 1.3 %collective-permute-start = (bf16[128,512]{1,0:T(8,128)(2,1)S(1)}, bf16[128,512]{1,0:T(8,128)(2,1)S(1)}, u32[]{:S(2)}, u32[]{:S(2)}) collective-permute-start(bf16[128,512]{1,0:T(8,128)(2,1)S(1)} %bitcast.4), channel_id=1, source_target_pairs={{0,1},{1,0},{2,3},{3,2},{4,5},{5,4},{6,7},{7,6},{8,9},{9,8},{10,11... | collective-permute-start | bytes 393224 | tf_op jit(solution)/shard_map/ppermute | solution.py:450

commit v4 on v3

--- a/solution.py
+++ b/solution.py
@@ -10,6 +10,7 @@
 
 EPSILON = 1e-05
 TINY = 1e-30
+MATRIX = 256
 F32 = jnp.float32
 BF16 = jnp.bfloat16
 TAP_PAD = 32
@@ -312,8 +313,16 @@
             offset += count
         halves = [split(jnp.maximum(piece, 0.0)) for piece in hidden]
         pair = jnp.concatenate([high for high, _ in halves] + [low for _, low in halves], axis=0)
-        partial = jnp.dot(second_ref[...], pair, preferred_element_type=F32)
+        deep = pair.shape[0]
+        cut = deep // MATRIX * MATRIX
+        if 2 * cut < deep:
+            cut = deep
+        partial = jnp.dot(second_ref[:, :cut], pair[:cut], preferred_element_type=F32)
         partial = partial[:partial_rows] + partial[partial_rows:]
+        if cut < deep:
+            partial = partial + jnp.dot(
+                second_ref[:partial_rows, cut:], pair[cut:], preferred_element_type=F32
+            )
         for side in range(rows):
             partial_ref[base + side + 1] = partial[:, side * columns : (side + 1) * columns]
 
@@ -347,12 +356,11 @@
     build(3, present(3))
 
     def step(device, most):
-        most = gather(device - 2, most)
+        layers(device)
         build(device + 2, present(device + 2))
-        layers(device)
-        return most
-
-    most = lax.fori_loop(2, devices, step, zero, unroll=2)
+        return gather(device - 2, most)
+
+    most = lax.fori_loop(2, devices, step, zero, unroll=min(14, devices - 2))
     most = gather(devices - 2, most)
     most = gather(devices - 1, most)
     best = jnp.max(most, axis=1, keepdims=True)

time: 45.8 us -> 43.9 us (0.959)
  Pallas kernels: 8.89 us -> 7.04 us
    pallas_call x1, Pallas kernels: 5.68 us -> 3.84 us  [shards(): pl.pallas_call(functools.partial(consensus_kernel, parts, local, rows), o...]
  transfers between devices with their start and end apart: 1 -> 1, of which waited for: 1 -> 1; matrix products, arithmetic and copies ran while one was open for 0% -> 0% of each run, Pallas kernels for 1% -> 2%
where the time goes in v4:
time: 43.9 us; the launch traced here: 43.6 us
  blocking collectives  35.7 us (81%)
  Pallas kernels  7.04 us (16%)
  waiting for transfers between devices  0.66 us (2%)
    all_to_all x3, blocking collectives, exchange(): return lax.all_to_all(slots, 'tgt', 0, 0, tiled=True)  35.7 us
    pallas_call x1, Pallas kernels, shards(): pl.pallas_call(functools.partial(consensus_kernel, parts, local, rows), o...  3.84 us
    pallas_call x1, Pallas kernels, shards(): pl.pallas_call(spread_kernel, out_shape=(jax.ShapeDtypeStruct((devices, s...  1.22 us
  transfers between devices with their start and end apart: 1, of which 1 were waited for; matrix products, arithmetic and copies ran while one was open for 0% of the time, Pallas kernels for 2%

profile of v4, /device:TPU:0, one launch (start us, length us, event | category | flops | bytes accessed | tf_op | source)
XLA Modules:
  0.0 43.6 jit_solution(402231713988266440)
XLA Ops:
  0.0 1.2 %spread.1 = (bf16[16,8,512]{2,1,0:T(8,128)(2,1)S(1)}, bf16[2,128,1024]{2,1,0:T(8,128)(2,1)S(1)}, bf16[64,2400]{1,0:T(8,128)(2,1)S(1)}, bf16[144,640]{1,0:T(8,128)(2,1)S(1)}) custom-call(bf16[8,1024]{1,0:T(8,128)(2,1)} %source_ref.1, bf16[2,128,1024]{2,1,0:T(8,128)(2,1)} %target_ref.1, bf16[64,2400]{1,0:T(8,128)(2,1)} %constant.4.clone.pick_ref, ...), custom_call_target="tpu_custom_call" | custom-call | tf_op jit(solution)/shard_map/spread/pallas_call | solution.py:435
  1.2 0.0 copy-start
  1.2 0.0 copy-start.1
  1.3 15.2 %all_to_all.15 = bf16[16,8,512]{2,1,0:T(8,128)(2,1)S(1)} all-to-all(bf16[16,8,512]{2,1,0:T(8,128)(2,1)S(1)} %get-tuple-element.12), channel_id=1, replica_groups=mesh['pairs'=2,'tgt'=16] {'tgt'}, dimensions={0} | all-to-all | bytes 262144 | tf_op jit(solution)/shard_map/all_to_all | solution.py:403
  16.5 0.0 collective-permute-start
  16.5 0.0 copy-done
  16.5 0.0 copy-done.1
  16.5 0.7 %prepare.1 = (bf16[256,1024]{1,0:T(8,128)(2,1)S(1)}, bf16[320,240]{1,0:T(8,128)(2,1)S(1)}, bf16[288,640]{1,0:T(8,128)(2,1)S(1)}) custom-call(bf16[2,128,1024]{2,1,0:T(8,128)(2,1)S(1)} %get-tuple-element.13.target_ref, f32[3,3,3,3,16]{4,3,2,1,0:T(4,128)S(1)} %bitcast.7, f32[3,3,3,3,16]{4,3,2,1,0:T(4,128)S(1)} %bitcast.8, ...), custom_call_target="tpu_custom_call" | custom-call | flops 1000000 | bytes 2000000 | tf_op jit(solution)/shard_map/prepare/pallas_call | solution.py:461
  17.2 0.7 %collective-permute-done.other_ref = bf16[128,512]{1,0:T(8,128)(2,1)S(1)} collective-permute-done((bf16[128,512]{1,0:T(8,128)(2,1)S(1)}, bf16[128,512]{1,0:T(8,128)(2,1)S(1)}, u32[]{:S(2)}, u32[]{:S(2)}) %collective-permute-start) | collective-permute-done | bytes 131104 | tf_op jit(solution)/shard_map/ppermute | solution.py:458
  17.9 0.5 %match.1 = f32[16,32,128]{2,1,0:T(8,128)S(1)} custom-call(bf16[128,512]{1,0:T(8,128)(2,1)S(1)} %bitcast.6, bf16[128,512]{1,0:T(8,128)(2,1)S(1)} %collective-permute-done.other_ref, bf16[256,1024]{1,0:T(8,128)(2,1)S(1)} %get-tuple-element.16.target_ref), custom_call_target="tpu_custom_call" | custom-call | tf_op jit(solution)/shard_map/match/pallas_call | solution.py:483
  18.4 10.5 %all_to_all.16 = f16[16,32,128]{2,1,0:T(8,128)(2,1)S(1)} all-to-all(f16[16,32,128]{2,1,0:T(8,128)(2,1)S(1)} %convert_element_type.12), channel_id=1, replica_groups=mesh['pairs'=2,'tgt'=16] {'tgt'}, dimensions={0} | all-to-all | bytes 262144 | tf_op jit(solution)/shard_map/all_to_all | solution.py:403
  28.9 3.8 %consensus.1 = f32[16,24,128]{2,1,0:T(8,128)S(1)} custom-call(f32[16,32,128]{2,1,0:T(8,128)S(1)} %convert_element_type.13.came_ref, bf16[320,240]{1,0:T(8,128)(2,1)S(1)} %get-tuple-element.17.first_ref, bf16[288,640]{1,0:T(8,128)(2,1)S(1)} %get-tuple-element.18.second_ref), custom_call_target="tpu_custom_call" | custom-call | tf_op jit(solution)/shard_map/consensus/pallas_call | solution.py:501
  32.7 10.0 %all_to_all.17 = f16[16,24,128]{2,1,0:T(8,128)(2,1)S(1)} all-to-all(f16[16,24,128]{2,1,0:T(8,128)(2,1)S(1)} %convert_element_type.14), channel_id=1, replica_groups=mesh['pairs'=2,'tgt'=16] {'tgt'}, dimensions={0} | all-to-all | bytes 196608 | tf_op jit(solution)/shard_map/all_to_all | solution.py:403
  42.7 0.9 %finish.1 = f32[128,2,128]{2,1,0:T(2,128)} custom-call(f32[16,24,128]{2,1,0:T(8,128)S(1)} %convert_element_type.15.came_ref), custom_call_target="tpu_custom_call" | custom-call | tf_op jit(solution)/shard_map/finish/pallas_call | solution.py:511
  (4 shorter events, 0.1 us)
Async XLA Ops:
  1.2 15.3 %copy-start = (f32[16,3,3,3,3]{0,4,3,2,1:T(4,128)S(1)}, f32[16,3,3,3,3]{0,4,3,2,1:T(4,128)}, u32[]{:S(2)}) copy-start(f32[16,3,3,3,3]{0,4,3,2,1:T(4,128)} %param.8) | copy-start | bytes 15556
  1.2 15.3 %copy-start.1 = (f32[16,3,3,3,3]{0,4,3,2,1:T(4,128)S(1)}, f32[16,3,3,3,3]{0,4,3,2,1:T(4,128)}, u32[]{:S(2)}) copy-start(f32[16,3,3,3,3]{0,4,3,2,1:T(4,128)} %param.9) | copy-start | bytes 15556
  16.5 1.3 %collective-permute-start = (bf16[128,512]{1,0:T(8,128)(2,1)S(1)}, bf16[128,512]{1,0:T(8,128)(2,1)S(1)}, u32[]{:S(2)}, u32[]{:S(2)}) collective-permute-start(bf16[128,512]{1,0:T(8,128)(2,1)S(1)} %bitcast.4), channel_id=1, source_target_pairs={{0,1},{1,0},{2,3},{3,2},{4,5},{5,4},{6,7},{7,6},{8,9},{9,8},{10,11... | collective-permute-start | bytes 393224 | tf_op jit(solution)/shard_map/ppermute | solution.py:458

commit v5 on v4

--- a/solution.py
+++ b/solution.py
@@ -13,6 +13,7 @@
 MATRIX = 256
 F32 = jnp.float32
 BF16 = jnp.bfloat16
+TAPS = 27
 TAP_PAD = 32
 SUBLANES = 8
 ORDER = ((0, 0), (1, 0), (2, 0), (0, 1), (1, 1), (2, 1))
@@ -34,37 +35,38 @@
     return parts
 
 
-def first_selector(parts):
-    tile = len(ORDER) * SUBLANES
-    width = 3 * (tile + REPEATED * SUBLANES)
-    blocks = [(first, hidden) for first, start, size in parts for hidden in range(start, start + size)]
-    select = np.zeros((2 * TAP_PAD, len(blocks), width), np.float32)
-    for number, (first, hidden) in enumerate(blocks):
-        for b in range(3):
-            for c in range(3):
-                for d in range(3):
-                    tap = (b * 3 + c) * 3 + d
-                    for place, (offset, low) in enumerate(ORDER):
-                        if offset != d:
-                            continue
-                        row = place * SUBLANES + hidden + b - first
-                        select[tap, number, c * tile + row] = 1
-                        if not low:
-                            column = 3 * tile + c * REPEATED * SUBLANES + row
-                            select[TAP_PAD + tap, number, column] = 1
-    return select.reshape(2 * TAP_PAD, -1)
-
-
-def second_selector(local):
-    select = np.zeros((3, 3, 2, SUBLANES, local + 2, 2, TAP_PAD), np.float32)
-    for b in range(3):
-        for c in range(3):
-            for d in range(3):
-                tap = (b * 3 + c) * 3 + d
-                for branch in range(2):
-                    for cell in range(local):
-                        select[c, d, branch, cell, cell + b, branch, tap] = 1
-    return select.reshape(18 * SUBLANES, -1)
+def tap_fields(tap):
+    return tap // 9, tap // 3 % 3, tap % 3
+
+
+def first_codes(width):
+    row = lax.broadcasted_iota(jnp.int32, (2 * TAP_PAD, 128), 0)
+    b, c, d = tap_fields(row % TAP_PAD)
+    rows = ((row // TAP_PAD * 3 + c) * 3 + d) * 16 + b
+    rows = jnp.where(row % TAP_PAD < TAPS, rows, -100)[:, :1]
+    column = lax.broadcasted_iota(jnp.int32, (SUBLANES, width), 1)
+    tile, again = len(ORDER) * SUBLANES, REPEATED * SUBLANES
+    extra = column >= 3 * tile
+    rest = column - 3 * tile
+    c = jnp.where(extra, rest // again, column // tile)
+    place = jnp.where(extra, rest % again, column % tile) // SUBLANES
+    code = ((jnp.where(extra, 3, 0) + c) * 3 + place % 3) * 16 + column % SUBLANES
+    columns = jnp.where(extra & (place >= 3), -1, code)[:1]
+    return rows, columns
+
+
+def second_selector(local, blocks):
+    height, width = 18 * SUBLANES, blocks * 2 * TAP_PAD
+    row = lax.broadcasted_iota(jnp.int32, (height, 128), 0)
+    rows = row // SUBLANES * 32 + row % SUBLANES
+    rows = jnp.where(row % SUBLANES < local, rows, -100)[:, :1]
+    column = lax.broadcasted_iota(jnp.int32, (SUBLANES, width), 1)
+    tap = column % TAP_PAD
+    b, c, d = tap_fields(tap)
+    cell = column // (2 * TAP_PAD) - b
+    code = ((c * 3 + d) * 2 + column // TAP_PAD % 2) * 32 + cell
+    columns = jnp.where((tap < TAPS) & (cell >= 0), code, -1)[:1]
+    return jnp.where(rows == columns, 1.0, 0.0).astype(BF16)
 
 
 def unit(features):
@@ -79,12 +81,8 @@
 
 
 def prepare_kernel(
-    devices, target_ref, first_ref, second_ref, pick_ref, spread_ref, gate_ref,
-    unit_ref, first_out, second_out, taps_ref,
+    devices, local, parts, first_ref, second_ref, gate_ref, first_out, second_out, taps_ref
 ):
-    rows, columns = target_ref.shape[:2]
-    for row in range(rows):
-        unit_ref[row * columns : (row + 1) * columns] = unit(target_ref[row])
     hid = first_ref.shape[-1]
     taps_ref[...] = jnp.zeros(taps_ref.shape, F32)
     for number, ref in enumerate((first_ref, second_ref)):
@@ -103,10 +101,12 @@
     width = first_out.shape[1]
     taps = jnp.concatenate(split(jnp.concatenate(branches[:2], axis=1)), axis=0)
     blocks = first_out.shape[0] // (2 * hid)
+    rows_code, columns_code = first_codes(width)
     for block in range(blocks):
+        first = [part[0] for part in parts if part[1] <= block][-1]
+        pick = jnp.where(rows_code + (block - first) == columns_code, 1.0, 0.0).astype(BF16)
         piece = lax.dot_general(
-            taps, pick_ref[:, block * width : (block + 1) * width],
-            (((0,), (0,)), ((), ())), preferred_element_type=F32,
+            taps, pick, (((0,), (0,)), ((), ())), preferred_element_type=F32
         )
         if block == 0:
             piece = piece * jnp.where(lax.axis_index("tgt") == 0, 0.0, 1.0)
@@ -122,26 +122,27 @@
     tiled = jnp.where(row_group == lane_group, tiled, 0.0)
     high, low = split(tiled)
     half = second_out.shape[0] // 2
-    high = jnp.dot(spread_ref[...], high, preferred_element_type=F32).astype(BF16)
-    low = jnp.dot(spread_ref[...], low, preferred_element_type=F32).astype(BF16)
+    scatter = second_selector(local, blocks)
+    high = jnp.dot(scatter, high, preferred_element_type=F32).astype(BF16)
+    low = jnp.dot(scatter, low, preferred_element_type=F32).astype(BF16)
     second_out[:half, :depth] = high
     second_out[:half, depth:] = high
     second_out[half:, :depth] = low
     second_out[half:, depth:] = jnp.zeros_like(low)
 
 
-def spread_kernel(
-    source_ref, target_ref, pick_ref, scatter_ref,
-    out_ref, target_out, pick_out, scatter_out, source_copy, sems,
-):
+def target_kernel(target_ref, gate_ref, unit_ref):
+    rows, columns = target_ref.shape[:2]
+    for row in range(rows):
+        unit_ref[row * columns : (row + 1) * columns] = unit(target_ref[row])
+
+
+def spread_kernel(source_ref, out_ref, source_copy, sems):
     copies = [
         pltpu.make_async_copy(start, end, sems.at[number])
         for number, (start, end) in enumerate(
             (
                 (source_ref, source_copy),
-                (target_ref, target_out),
-                (pick_ref, pick_out),
-                (scatter_ref, scatter_out),
             )
         )
     ]
@@ -430,55 +431,55 @@
     depth = hidden * 2 * hid
     assert local <= SUBLANES and rows * devices % 4 == 0
 
-    pick = jnp.asarray(first_selector(parts), BF16)
-    scatter = jnp.asarray(second_selector(local), BF16)
-    spread, target_features, pick, scatter = pl.pallas_call(
+    (spread,) = pl.pallas_call(
         spread_kernel,
         out_shape=(
             jax.ShapeDtypeStruct((devices, source_features.shape[0], channels // 2), BF16),
-            jax.ShapeDtypeStruct(target_features.shape, BF16),
-            jax.ShapeDtypeStruct(pick.shape, BF16),
-            jax.ShapeDtypeStruct(scatter.shape, BF16),
         ),
-        in_specs=[ANY] * 4,
-        out_specs=(VMEM,) * 4,
+        in_specs=[ANY] * 1,
+        out_specs=(VMEM,) * 1,
         scratch_shapes=[
             pltpu.VMEM(source_features.shape, BF16),
-            pltpu.SemaphoreType.DMA((4,)),
+            pltpu.SemaphoreType.DMA((1,)),
         ],
         compiler_params=room(),
         name="spread",
     )(
         *(
             pltpu.with_memory_space_constraint(value, pltpu.HBM)
-            for value in (source_features, target_features, pick, scatter)
+            for value in (source_features,)
         )
     )
     mine = exchange(spread).reshape(cells, channels // 2)
     other = lax.ppermute(mine, "tgt", [(i, i ^ 1) for i in range(devices)])
 
     second_rows = 18 * SUBLANES
-    target_unit, first_weights, second_weights = pl.pallas_call(
-        functools.partial(prepare_kernel, devices),
+    first_weights, second_weights = pl.pallas_call(
+        functools.partial(prepare_kernel, devices, local, parts),
         out_shape=(
-            jax.ShapeDtypeStruct((rows * columns, channels), BF16),
             jax.ShapeDtypeStruct((depth, width), BF16),
             jax.ShapeDtypeStruct((2 * second_rows, 2 * depth), BF16),
         ),
-        in_specs=[VMEM] * 5 + [pl.BlockSpec(memory_space=pl.ANY)],
-        out_specs=(VMEM,) * 3,
+        in_specs=[VMEM] * 2 + [pl.BlockSpec(memory_space=pl.ANY)],
+        out_specs=(VMEM,) * 2,
         scratch_shapes=[pltpu.VMEM((4 * TAP_PAD, 128), F32)],
-        cost_estimate=pl.CostEstimate(flops=10**6, bytes_accessed=2 * 10**6, transcendentals=0),
+        cost_estimate=pl.CostEstimate(flops=10**9, bytes_accessed=10**6, transcendentals=0),
         compiler_params=room(),
         name="prepare",
     )(
-        target_features,
         jnp.transpose(conv_first, (1, 2, 3, 4, 0)),
         jnp.transpose(conv_second, (1, 2, 3, 4, 0)),
-        pick,
-        scatter,
         mine,
     )
+    target_unit = pl.pallas_call(
+        target_kernel,
+        out_shape=jax.ShapeDtypeStruct((rows * columns, channels), BF16),
+        in_specs=[VMEM, pl.BlockSpec(memory_space=pl.ANY)],
+        out_specs=VMEM,
+        cost_estimate=pl.CostEstimate(flops=10**6, bytes_accessed=10**6, transcendentals=0),
+        compiler_params=room(),
+        name="target",
+    )(target_features, first_weights)
 
     slots = pl.pallas_call(
         functools.partial(match_kernel, local),

time: 43.9 us -> 43.4 us (0.989)
  waiting for transfers between devices: 0.66 us -> 0.05 us
    ppermute x1, waiting for transfers between devices: 0.66 us -> 0.05 us  [shards(): other = lax.ppermute(mine, 'tgt', [(i, i ^ 1) for i in range(devices)])]
    pallas_call x1, Pallas kernels: 1.22 us -> 0.73 us  [shards(): pl.pallas_call(spread_kernel, out_shape=(jax.ShapeDtypeStruct((devices, s...]
    pallas_call x1 -> x2, Pallas kernels: 0.67 us -> 0.9 us  [the longest x1 0.66 us: shards(): pl.pallas_call(functools.partial(prepare_kernel, devices, local, parts),...]
  transfers between devices with their start and end apart: 1 -> 1, of which waited for: 1 -> 0; matrix products, arithmetic and copies ran while one was open for 0% -> 0% of each run, Pallas kernels for 2% -> 2%
where the time goes in v5:
time: 43.4 us; the launch traced here: 43.1 us
  blocking collectives  35.7 us (82%)
  Pallas kernels  6.77 us (16%)
    all_to_all x3, blocking collectives, exchange(): return lax.all_to_all(slots, 'tgt', 0, 0, tiled=True)  35.7 us
    pallas_call x1, Pallas kernels, shards(): pl.pallas_call(functools.partial(consensus_kernel, parts, local, rows), o...  3.83 us
  transfers between devices with their start and end apart: 1, of which 0 were waited for; matrix products, arithmetic and copies ran while one was open for 0% of the time, Pallas kernels for 2%

profile of v5, /device:TPU:0, one launch (start us, length us, event | category | flops | bytes accessed | tf_op | source)
XLA Modules:
  0.0 43.1 jit_solution(9167139509602132285)
XLA Ops:
  0.0 0.7 %spread.1 = bf16[16,8,512]{2,1,0:T(8,128)(2,1)S(1)} custom-call(bf16[8,1024]{1,0:T(8,128)(2,1)} %source_ref.1), custom_call_target="tpu_custom_call" | custom-call | tf_op jit(solution)/shard_map/spread/pallas_call | solution.py:434
  0.7 0.0 copy-start.1
  0.8 0.0 copy-start.2
  0.8 15.2 %all_to_all.15 = bf16[16,8,512]{2,1,0:T(8,128)(2,1)S(1)} all-to-all(bf16[16,8,512]{2,1,0:T(8,128)(2,1)S(1)} %spread.1), channel_id=1, replica_groups=mesh['pairs'=2,'tgt'=16] {'tgt'}, dimensions={0} | all-to-all | bytes 262144 | tf_op jit(solution)/shard_map/all_to_all | solution.py:404
  16.0 0.0 collective-permute-start
  16.0 0.0 copy-done.1
  16.0 0.0 copy-done.2
  16.0 0.0 copy-start
  16.0 0.7 %prepare.1 = (bf16[320,240]{1,0:T(8,128)(2,1)S(1)}, bf16[288,640]{1,0:T(8,128)(2,1)S(1)}) custom-call(f32[3,3,3,3,16]{4,3,2,1,0:T(4,128)S(1)} %bitcast.7, f32[3,3,3,3,16]{4,3,2,1,0:T(4,128)S(1)} %bitcast.8, bf16[128,512]{1,0:T(8,128)(2,1)S(1)} %bitcast.5), custom_call_target="tpu_custom_call" | custom-call | flops 1000000000 | bytes 1000000 | tf_op jit(solution)/shard_map/prepare/pallas_call | solution.py:457
  16.7 0.4 copy-done
  17.1 0.2 target.1.target_ref
  17.3 0.0 collective-permute-done.other_ref
  17.4 0.5 %match.1 = f32[16,32,128]{2,1,0:T(8,128)S(1)} custom-call(bf16[128,512]{1,0:T(8,128)(2,1)S(1)} %bitcast.6, bf16[128,512]{1,0:T(8,128)(2,1)S(1)} %collective-permute-done.other_ref, bf16[256,1024]{1,0:T(8,128)(2,1)S(1)} %target.1.target_ref), custom_call_target="tpu_custom_call" | custom-call | tf_op jit(solution)/shard_map/match/pallas_call | solution.py:484
  17.9 10.5 %all_to_all.16 = f16[16,32,128]{2,1,0:T(8,128)(2,1)S(1)} all-to-all(f16[16,32,128]{2,1,0:T(8,128)(2,1)S(1)} %convert_element_type.12), channel_id=1, replica_groups=mesh['pairs'=2,'tgt'=16] {'tgt'}, dimensions={0} | all-to-all | bytes 262144 | tf_op jit(solution)/shard_map/all_to_all | solution.py:404
  28.4 3.8 %consensus.1 = f32[16,24,128]{2,1,0:T(8,128)S(1)} custom-call(f32[16,32,128]{2,1,0:T(8,128)S(1)} %convert_element_type.13.came_ref, bf16[320,240]{1,0:T(8,128)(2,1)S(1)} %get-tuple-element.7.gate_ref.first_ref, bf16[288,640]{1,0:T(8,128)(2,1)S(1)} %get-tuple-element.8.second_ref), custom_call_target="tpu_custom_call" | custom-call | tf_op jit(solution)/shard_map/consensus/pallas_call | solution.py:502
  32.2 10.0 %all_to_all.17 = f16[16,24,128]{2,1,0:T(8,128)(2,1)S(1)} all-to-all(f16[16,24,128]{2,1,0:T(8,128)(2,1)S(1)} %convert_element_type.14), channel_id=1, replica_groups=mesh['pairs'=2,'tgt'=16] {'tgt'}, dimensions={0} | all-to-all | bytes 196608 | tf_op jit(solution)/shard_map/all_to_all | solution.py:404
  42.2 0.9 %finish.1 = f32[128,2,128]{2,1,0:T(2,128)} custom-call(f32[16,24,128]{2,1,0:T(8,128)S(1)} %convert_element_type.15.came_ref), custom_call_target="tpu_custom_call" | custom-call | tf_op jit(solution)/shard_map/finish/pallas_call | solution.py:512
  (4 shorter events, 0.1 us)
Async XLA Ops:
  0.7 15.3 %copy-start.1 = (f32[16,3,3,3,3]{0,4,3,2,1:T(4,128)S(1)}, f32[16,3,3,3,3]{0,4,3,2,1:T(4,128)}, u32[]{:S(2)}) copy-start(f32[16,3,3,3,3]{0,4,3,2,1:T(4,128)} %param.6) | copy-start | bytes 15556
  0.8 15.3 %copy-start.2 = (f32[16,3,3,3,3]{0,4,3,2,1:T(4,128)S(1)}, f32[16,3,3,3,3]{0,4,3,2,1:T(4,128)}, u32[]{:S(2)}) copy-start(f32[16,3,3,3,3]{0,4,3,2,1:T(4,128)} %param.7) | copy-start | bytes 15556
  16.0 1.3 %collective-permute-start = (bf16[128,512]{1,0:T(8,128)(2,1)S(1)}, bf16[128,512]{1,0:T(8,128)(2,1)S(1)}, u32[]{:S(2)}, u32[]{:S(2)}) collective-permute-start(bf16[128,512]{1,0:T(8,128)(2,1)S(1)} %bitcast.4), channel_id=1, source_target_pairs={{0,1},{1,0},{2,3},{3,2},{4,5},{5,4},{6,7},{7,6},{8,9},{9,8},{10,11... | collective-permute-start | bytes 393224 | tf_op jit(solution)/shard_map/ppermute | solution.py:454
  16.0 1.0 %copy-start = (bf16[2,128,1024]{2,1,0:T(8,128)(2,1)S(1)}, bf16[2,128,1024]{2,1,0:T(8,128)(2,1)}, u32[]{:S(2)}) copy-start(bf16[2,128,1024]{2,1,0:T(8,128)(2,1)} %target_ref.1) | copy-start | bytes 1572868

commit v6 on v5

--- a/solution.py
+++ b/solution.py
@@ -11,6 +11,7 @@
 EPSILON = 1e-05
 TINY = 1e-30
 MATRIX = 256
+UNROLLED = 16
 F32 = jnp.float32
 BF16 = jnp.bfloat16
 TAPS = 27
@@ -238,7 +239,7 @@
 
 
 def consensus_kernel(
-    parts, local, rows, came_ref, first_ref, second_ref, send_ref, tile_ref, partial_ref, rows_ref
+    parts, local, rows, came_ref, first_ref, second_ref, send_ref, tile_ref, partial_ref, rows_ref, pair_ref
 ):
     devices, _, columns = came_ref.shape
     window = max(SUBLANES, local + 4)
@@ -272,10 +273,15 @@
     for number in range(len(parts)):
         tile_ref[0, number] = blank
 
-    def build(device, present):
-        source = jnp.minimum(device, devices - 1)
+    def build(device):
+        if isinstance(device, int) and device == devices:
+            for row in range(rows):
+                for number in range(len(parts)):
+                    tile_ref[device * rows + row + 1, number] = blank
+            return
+        source = device
         for row in range(rows):
-            inverse = rows_ref[source * rows + row, window : window + 1, :] * present
+            inverse = rows_ref[source * rows + row, window : window + 1, :]
             for number, (first, _, _) in enumerate(parts):
                 value = piece_of(source, row, first)
                 value = value * (value * inverse) * (value * scales[number])
@@ -293,7 +299,7 @@
     partial_ref[0] = empty
     partial_ref[grid_rows + 1] = empty
 
-    def layers(device):
+    def layer_one(device):
         base = device * rows
         hidden = []
         offset = 0
@@ -312,8 +318,18 @@
                 )
             )
             offset += count
-        halves = [split(jnp.maximum(piece, 0.0)) for piece in hidden]
-        pair = jnp.concatenate([high for high, _ in halves] + [low for _, low in halves], axis=0)
+        place = 0
+        deep = pair_ref.shape[1] // 2
+        for piece in hidden:
+            high, low = split(jnp.maximum(piece, 0.0))
+            size = piece.shape[0]
+            pair_ref[device % 2, place : place + size] = high
+            pair_ref[device % 2, deep + place : deep + place + size] = low
+            place += size
+
+    def layer_two(device):
+        base = device * rows
+        pair = pair_ref[device % 2]
         deep = pair.shape[0]
         cut = deep // MATRIX * MATRIX
         if 2 * cut < deep:
@@ -346,24 +362,29 @@
             most = jnp.maximum(most, total)
         return most
 
-    def present(device):
-        return jnp.where(device < devices, 1.0, 0.0).astype(F32)
-
-    build(0, 1.0)
-    build(1, 1.0)
-    layers(0)
-    build(2, present(2))
-    layers(1)
-    build(3, present(3))
-
     def step(device, most):
-        layers(device)
-        build(device + 2, present(device + 2))
-        return gather(device - 2, most)
-
-    most = lax.fori_loop(2, devices, step, zero, unroll=min(14, devices - 2))
-    most = gather(devices - 2, most)
-    most = gather(devices - 1, most)
+        fixed = isinstance(device, int)
+        if not fixed or device + 1 < devices:
+            layer_one(device + 1)
+        if not fixed or device >= 2:
+            most = gather(device - 2, most)
+        if not fixed or device + 3 <= devices:
+            build(device + 3)
+        layer_two(device)
+        return most
+
+    for device in range(3):
+        build(device)
+    layer_one(0)
+    most = zero
+    ahead, behind = (2, 3) if devices > UNROLLED else (devices, 0)
+    for device in range(ahead):
+        most = step(device, most)
+    most = lax.fori_loop(ahead, devices - behind, step, most) if behind else most
+    for device in range(devices - behind, devices):
+        most = step(device, most)
+    for device in range(devices - 2, devices):
+        most = gather(device, most)
     best = jnp.max(most, axis=1, keepdims=True)
     scale = 1.0 / jnp.maximum(best, TINY)
     root = jnp.concatenate(
@@ -495,9 +516,10 @@
     )(mine, other, target_unit)
 
     stores = (
-        ((rows * (devices + 2) + 2, len(parts), tile, columns), BF16),
+        ((rows * (devices + 1) + 1, len(parts), tile, columns), BF16),
         ((rows * devices + 2, second_rows, columns), F32),
         ((rows * devices, whole_tiles(window + 1), columns), F32),
+        ((2, 2 * depth, rows * columns), BF16),
     )
     slots = pl.pallas_call(
         functools.partial(consensus_kernel, parts, local, rows),

time: 43.4 us -> 42.7 us (0.984)
  Pallas kernels: 6.77 us -> 6 us
    pallas_call x1, Pallas kernels: 3.83 us -> 3.06 us  [shards(): pl.pallas_call(functools.partial(consensus_kernel, parts, local, rows), o...]
where the time goes in v6:
time: 42.7 us; the launch traced here: 42.3 us
  blocking collectives  35.7 us (84%)
  Pallas kernels  6 us (14%)
    all_to_all x3, blocking collectives, exchange(): return lax.all_to_all(slots, 'tgt', 0, 0, tiled=True)  35.7 us
    pallas_call x1, Pallas kernels, shards(): pl.pallas_call(functools.partial(consensus_kernel, parts, local, rows), o...  3.06 us
    pallas_call x1, Pallas kernels, shards(): pl.pallas_call(functools.partial(finish_kernel, local), out_shape=jax.Sha...  0.86 us
  transfers between devices with their start and end apart: 1, of which 0 were waited for; matrix products, arithmetic and copies ran while one was open for 0% of the time, Pallas kernels for 2%

profile of v6, /device:TPU:0, one launch (start us, length us, event | category | flops | bytes accessed | tf_op | source)
XLA Modules:
  0.0 42.3 jit_solution(14492820365895688624)
XLA Ops:
  0.0 0.7 %spread.1 = bf16[16,8,512]{2,1,0:T(8,128)(2,1)S(1)} custom-call(bf16[8,1024]{1,0:T(8,128)(2,1)} %source_ref.1), custom_call_target="tpu_custom_call" | custom-call | tf_op jit(solution)/shard_map/spread/pallas_call | solution.py:455
  0.7 0.0 copy-start.1
  0.8 0.0 copy-start.2
  0.8 15.2 %all_to_all.15 = bf16[16,8,512]{2,1,0:T(8,128)(2,1)S(1)} all-to-all(bf16[16,8,512]{2,1,0:T(8,128)(2,1)S(1)} %spread.1), channel_id=1, replica_groups=mesh['pairs'=2,'tgt'=16] {'tgt'}, dimensions={0} | all-to-all | bytes 262144 | tf_op jit(solution)/shard_map/all_to_all | solution.py:425
  16.0 0.0 collective-permute-start
  16.0 0.0 copy-done.1
  16.0 0.0 copy-done.2
  16.0 0.0 copy-start
  16.0 0.7 %prepare.1 = (bf16[320,240]{1,0:T(8,128)(2,1)S(1)}, bf16[288,640]{1,0:T(8,128)(2,1)S(1)}) custom-call(f32[3,3,3,3,16]{4,3,2,1,0:T(4,128)S(1)} %bitcast.7, f32[3,3,3,3,16]{4,3,2,1,0:T(4,128)S(1)} %bitcast.8, bf16[128,512]{1,0:T(8,128)(2,1)S(1)} %bitcast.5), custom_call_target="tpu_custom_call" | custom-call | flops 1000000000 | bytes 1000000 | tf_op jit(solution)/shard_map/prepare/pallas_call | solution.py:478
  16.7 0.4 copy-done
  17.1 0.2 target.1.target_ref
  17.3 0.0 collective-permute-done.other_ref
  17.4 0.5 %match.1 = f32[16,32,128]{2,1,0:T(8,128)S(1)} custom-call(bf16[128,512]{1,0:T(8,128)(2,1)S(1)} %bitcast.6, bf16[128,512]{1,0:T(8,128)(2,1)S(1)} %collective-permute-done.other_ref, bf16[256,1024]{1,0:T(8,128)(2,1)S(1)} %target.1.target_ref), custom_call_target="tpu_custom_call" | custom-call | tf_op jit(solution)/shard_map/match/pallas_call | solution.py:505
  17.9 10.5 %all_to_all.16 = f16[16,32,128]{2,1,0:T(8,128)(2,1)S(1)} all-to-all(f16[16,32,128]{2,1,0:T(8,128)(2,1)S(1)} %convert_element_type.12), channel_id=1, replica_groups=mesh['pairs'=2,'tgt'=16] {'tgt'}, dimensions={0} | all-to-all | bytes 262144 | tf_op jit(solution)/shard_map/all_to_all | solution.py:425
  28.4 3.1 %consensus.1 = f32[16,24,128]{2,1,0:T(8,128)S(1)} custom-call(f32[16,32,128]{2,1,0:T(8,128)S(1)} %convert_element_type.13.came_ref, bf16[320,240]{1,0:T(8,128)(2,1)S(1)} %get-tuple-element.7.gate_ref.first_ref, bf16[288,640]{1,0:T(8,128)(2,1)S(1)} %get-tuple-element.8.second_ref), custom_call_target="tpu_custom_call" | custom-call | tf_op jit(solution)/shard_map/consensus/pallas_call | solution.py:524
  31.5 10.0 %all_to_all.17 = f16[16,24,128]{2,1,0:T(8,128)(2,1)S(1)} all-to-all(f16[16,24,128]{2,1,0:T(8,128)(2,1)S(1)} %convert_element_type.14), channel_id=1, replica_groups=mesh['pairs'=2,'tgt'=16] {'tgt'}, dimensions={0} | all-to-all | bytes 196608 | tf_op jit(solution)/shard_map/all_to_all | solution.py:425
  41.5 0.9 %finish.1 = f32[128,2,128]{2,1,0:T(2,128)} custom-call(f32[16,24,128]{2,1,0:T(8,128)S(1)} %convert_element_type.15.came_ref), custom_call_target="tpu_custom_call" | custom-call | tf_op jit(solution)/shard_map/finish/pallas_call | solution.py:534
  (4 shorter events, 0.1 us)
Async XLA Ops:
  0.7 15.3 %copy-start.1 = (f32[16,3,3,3,3]{0,4,3,2,1:T(4,128)S(1)}, f32[16,3,3,3,3]{0,4,3,2,1:T(4,128)}, u32[]{:S(2)}) copy-start(f32[16,3,3,3,3]{0,4,3,2,1:T(4,128)} %param.6) | copy-start | bytes 15556
  0.8 15.3 %copy-start.2 = (f32[16,3,3,3,3]{0,4,3,2,1:T(4,128)S(1)}, f32[16,3,3,3,3]{0,4,3,2,1:T(4,128)}, u32[]{:S(2)}) copy-start(f32[16,3,3,3,3]{0,4,3,2,1:T(4,128)} %param.7) | copy-start | bytes 15556
  16.0 1.3 %collective-permute-start = (bf16[128,512]{1,0:T(8,128)(2,1)S(1)}, bf16[128,512]{1,0:T(8,128)(2,1)S(1)}, u32[]{:S(2)}, u32[]{:S(2)}) collective-permute-start(bf16[128,512]{1,0:T(8,128)(2,1)S(1)} %bitcast.4), channel_id=1, source_target_pairs={{0,1},{1,0},{2,3},{3,2},{4,5},{5,4},{6,7},{7,6},{8,9},{9,8},{10,11... | collective-permute-start | bytes 393224 | tf_op jit(solution)/shard_map/ppermute | solution.py:475
  16.0 1.0 %copy-start = (bf16[2,128,1024]{2,1,0:T(8,128)(2,1)S(1)}, bf16[2,128,1024]{2,1,0:T(8,128)(2,1)}, u32[]{:S(2)}) copy-start(bf16[2,128,1024]{2,1,0:T(8,128)(2,1)} %target_ref.1) | copy-start | bytes 1572868

commit v7 on v6

--- a/solution.py
+++ b/solution.py
@@ -138,55 +138,30 @@
         unit_ref[row * columns : (row + 1) * columns] = unit(target_ref[row])
 
 
-def spread_kernel(source_ref, out_ref, source_copy, sems):
-    copies = [
-        pltpu.make_async_copy(start, end, sems.at[number])
-        for number, (start, end) in enumerate(
-            (
-                (source_ref, source_copy),
-            )
-        )
-    ]
-    for copy in copies:
-        copy.start()
-    copies[0].wait()
-    half = out_ref.shape[2]
-    for device in range(out_ref.shape[0]):
-        start = device % 2 * half
-        out_ref[device] = source_copy[:, start : start + half]
-    for copy in copies[1:]:
-        copy.wait()
-
-
 def match_kernel(
-    local, mine_ref, other_ref, target_ref, send_ref, source_ref, order_ref
+    local, masks, near_ref, far_ref, target_ref, send_ref, source_ref, order_ref
 ):
     rows, padded, columns = order_ref.shape
     cells = padded - 2 * SUBLANES
-    half = mine_ref.shape[1]
-    side = lax.axis_index("tgt") % 2
-    block = min(cells, 32)
-    for first in range(0, cells, block):
-        halves = [
-            jnp.maximum(ref[first : first + block].astype(F32), 0.0)
-            for ref in (mine_ref, other_ref)
-        ]
-        squares = [jnp.sum(piece * piece, axis=-1, keepdims=True) for piece in halves]
-        length = jnp.sqrt(squares[0] + squares[1] + 1e-06)
-        for number, piece in enumerate(halves):
-            start = pl.multiple_of((side ^ number) * half, half)
-            source_ref[first : first + block, pl.ds(start, half)] = (piece / length).astype(BF16)
+    middle = near_ref.shape[0]
+    source_ref[:middle] = unit(near_ref[...])
+    source_ref[middle:] = unit(far_ref[...])
     correlation = lax.dot_general(
         source_ref[...], target_ref[...], (((1,), (1,)), ((), ())), preferred_element_type=F32
     )
+    position = lax.axis_index("tgt")
     window = max(SUBLANES, local + 4)
     blank = jnp.zeros((SUBLANES, columns), F32)
     for row in range(rows):
         order_ref[row, :SUBLANES, :] = blank
         order_ref[row, SUBLANES + cells :, :] = blank
-        order_ref[row, SUBLANES : SUBLANES + cells, :] = correlation[
-            :, row * columns : (row + 1) * columns
-        ]
+        for piece, mask in enumerate(masks):
+            start = SUBLANES + (position ^ mask) * local
+            if local % SUBLANES == 0:
+                start = pl.multiple_of(start, SUBLANES)
+            order_ref[row, pl.ds(start, local), :] = correlation[
+                piece * local : (piece + 1) * local, row * columns : (row + 1) * columns
+            ]
         source_best = jnp.max(order_ref[row], axis=0, keepdims=True)
         scale = 1.0 / jnp.maximum(source_best, TINY)
         root = jnp.concatenate(root_rows(source_best), axis=0)
@@ -421,6 +396,29 @@
             out_ref[device * local : (device + 1) * local, row, :] = value[:local]
 
 
+def gather_sources(value, devices):
+    bits = []
+    bit = 1
+    while bit < devices:
+        bits.append(bit)
+        bit *= 2
+    upper = bits[2:]
+    stages = [[2]]
+    for first in range(0, len(upper), 2):
+        pair = upper[first : first + 2]
+        stages.append(pair if len(pair) == 1 else [pair[0], pair[0] ^ pair[1], pair[1]])
+    masks = [0]
+    gate = None
+    for stage in stages:
+        parts = [value] + [
+            lax.ppermute(value, "tgt", [(i, i ^ mask) for i in range(devices)]) for mask in stage
+        ]
+        value = jnp.concatenate(parts, axis=0)
+        masks = [mask ^ extra for extra in [0] + stage for mask in masks]
+        gate = value if gate is None else gate
+    return value, masks + [mask ^ 1 for mask in masks], gate
+
+
 def exchange(slots):
     return lax.all_to_all(slots, "tgt", 0, 0, tiled=True)
 
@@ -435,7 +433,6 @@
 
 
 VMEM = pl.BlockSpec(memory_space=pltpu.VMEM)
-ANY = pl.BlockSpec(memory_space=pltpu.HBM)
 
 
 def shards(source_features, target_features, conv_first, conv_second):
@@ -452,27 +449,7 @@
     depth = hidden * 2 * hid
     assert local <= SUBLANES and rows * devices % 4 == 0
 
-    (spread,) = pl.pallas_call(
-        spread_kernel,
-        out_shape=(
-            jax.ShapeDtypeStruct((devices, source_features.shape[0], channels // 2), BF16),
-        ),
-        in_specs=[ANY] * 1,
-        out_specs=(VMEM,) * 1,
-        scratch_shapes=[
-            pltpu.VMEM(source_features.shape, BF16),
-            pltpu.SemaphoreType.DMA((1,)),
-        ],
-        compiler_params=room(),
-        name="spread",
-    )(
-        *(
-            pltpu.with_memory_space_constraint(value, pltpu.HBM)
-            for value in (source_features,)
-        )
-    )
-    mine = exchange(spread).reshape(cells, channels // 2)
-    other = lax.ppermute(mine, "tgt", [(i, i ^ 1) for i in range(devices)])
+    near, masks, mine = gather_sources(source_features, devices)
 
     second_rows = 18 * SUBLANES
     first_weights, second_weights = pl.pallas_call(
@@ -502,8 +479,12 @@
         name="target",
     )(target_features, first_weights)
 
+    near, target_unit, first_weights = lax.optimization_barrier(
+        (near, target_unit, first_weights)
+    )
+    far = lax.ppermute(near, "tgt", [(i, i ^ 1) for i in range(devices)])
     slots = pl.pallas_call(
-        functools.partial(match_kernel, local),
+        functools.partial(match_kernel, local, masks),
         out_shape=jax.ShapeDtypeStruct((devices, whole_tiles(rows * (window + 2)), columns), F32),
         in_specs=[VMEM] * 3,
         out_specs=VMEM,
@@ -513,7 +494,7 @@
         ],
         compiler_params=room(),
         name="match",
-    )(mine, other, target_unit)
+    )(near, far, target_unit)
 
     stores = (
         ((rows * (devices + 1) + 1, len(parts), tile, columns), BF16),

time: 42.7 us -> 42.1 us (0.986)
  blocking collectives: 35.7 us -> 22.1 us
  starting transfers between devices: 0.01 us -> 7.74 us
  waiting for transfers between devices: 0.05 us -> 4.53 us
  local copies, waits for them, and re-layouts: 0.38 us -> 1.95 us
  Pallas kernels: 6 us -> 5.35 us
    all_to_all x3 -> x2, blocking collectives: 35.7 us -> 22.1 us  [exchange(): return lax.all_to_all(slots, 'tgt', 0, 0, tiled=True)]
    ppermute x1 -> x5, starting transfers between devices: 0.01 us -> 7.74 us  [the longest x4 7.67 us: gather_sources(): lax.ppermute(value, 'tgt', [(i, i ^ mask) for i in range(devices)])]
    ppermute x1 -> x5, waiting for transfers between devices: 0.05 us -> 4.53 us  [the longest x4 3.2 us: gather_sources(): lax.ppermute(value, 'tgt', [(i, i ^ mask) for i in range(devices)])]
    unnamed x6 -> x9, local copies, waits for them, and re-layouts: 0.38 us -> 1.95 us
    pallas_call x2 -> x1, Pallas kernels: 1.19 us -> 0.44 us  [shards(): pl.pallas_call(functools.partial(match_kernel, local, masks), out_shape=j...]
  transfers between devices with their start and end apart: 1 -> 5, of which waited for: 0 -> 4; matrix products, arithmetic and copies ran while one was open for 0% -> 2% of each run, Pallas kernels for 2% -> 2%
where the time goes in v7:
time: 42.1 us; the launch traced here: 41.8 us
  blocking collectives  22.1 us (52%)
  starting transfers between devices  7.74 us (18%)
  Pallas kernels  5.35 us (13%)
  waiting for transfers between devices  4.53 us (11%)
  local copies, waits for them, and re-layouts  1.95 us (5%)
    all_to_all x2, blocking collectives, exchange(): return lax.all_to_all(slots, 'tgt', 0, 0, tiled=True)  22.1 us
    ppermute x4, starting transfers between devices, gather_sources(): lax.ppermute(value, 'tgt', [(i, i ^ mask) for i in range(devices)])  7.67 us
    ppermute x4, waiting for transfers between devices, gather_sources(): lax.ppermute(value, 'tgt', [(i, i ^ mask) for i in range(devices)])  3.2 us
    pallas_call x1, Pallas kernels, shards(): pl.pallas_call(functools.partial(consensus_kernel, parts, local, rows), o...  3.16 us
    unnamed x9, local copies, waits for them, and re-layouts  1.95 us
    ppermute x1, waiting for transfers between devices, shards(): far = lax.ppermute(near, 'tgt', [(i, i ^ 1) for i in range(devices)])  1.33 us
    pallas_call x1, Pallas kernels, shards(): pl.pallas_call(functools.partial(finish_kernel, local), out_shape=jax.Sha...  0.86 us
  transfers between devices with their start and end apart: 5, of which 4 were waited for; matrix products, arithmetic and copies ran while one was open for 2% of the time, Pallas kernels for 2%

profile of v7, /device:TPU:0, one launch (start us, length us, event | category | flops | bytes accessed | tf_op | source)
XLA Modules:
  0.0 41.8 jit_solution(18109736957179196033)
XLA Ops:
  0.0 0.0 copy-start.1
  0.0 3.0 %collective-permute-start = (bf16[8,1024]{1,0:T(8,128)(2,1)}, bf16[8,1024]{1,0:T(8,128)(2,1)S(1)}, u32[]{:S(2)}, u32[]{:S(2)}) collective-permute-start(bf16[8,1024]{1,0:T(8,128)(2,1)} %param.4), channel_id=1, source_target_pairs={{0,2},{1,3},{2,0},{3,1},{4,6},{5,7},{6,4},{7,5},{8,10},{9,11},{10,... | collective-permute-start | bytes 49160 | tf_op jit(solution)/shard_map/ppermute | solution.py:414
  3.0 0.8 %constant_dynamic-update-slice_fusion.1 = (bf16[16,1024]{1,0:T(8,128)(2,1)S(1)}, bf16[64,1024]{1,0:T(8,128)(2,1)S(1)}) fusion(bf16[8,1024]{1,0:T(8,128)(2,1)} %param.4), kind=kLoop, calls=%fused_computation.1 | loop fusion | bytes 49152
  3.8 1.2 %collective-permute-done = bf16[8,1024]{1,0:T(8,128)(2,1)S(1)} collective-permute-done((bf16[8,1024]{1,0:T(8,128)(2,1)}, bf16[8,1024]{1,0:T(8,128)(2,1)S(1)}, u32[]{:S(2)}, u32[]{:S(2)}) %collective-permute-start) | collective-permute-done | bytes 16416 | tf_op jit(solution)/shard_map/ppermute | solution.py:414
  4.9 3.1 %collective-permute-start.3 = (bf16[16,1024]{1,0:T(8,128)(2,1)S(1)}, bf16[16,1024]{1,0:T(8,128)(2,1)S(1)}, u32[]{:S(2)}, u32[]{:S(2)}) collective-permute-start(bf16[16,1024]{1,0:T(8,128)(2,1)S(1)} %get-tuple-element.15.gate_ref), channel_id=1, source_target_pairs={{0,8},{1,9},{2,10},{3,11},{4,12},{5,13},{6,14},{7,15},{8,0},{9,1},... | collective-permute-start | bytes 98312 | tf_op jit(solution)/shard_map/ppermute | solution.py:414
  8.0 1.3 %collective-permute-start.2 = (bf16[16,1024]{1,0:T(8,128)(2,1)S(1)}, bf16[16,1024]{1,0:T(8,128)(2,1)S(1)}, u32[]{:S(2)}, u32[]{:S(2)}) collective-permute-start(bf16[16,1024]{1,0:T(8,128)(2,1)S(1)} %get-tuple-element.15.gate_ref), channel_id=1, source_target_pairs={{0,12},{1,13},{2,14},{3,15},{4,8},{5,9},{6,10},{7,11},{8,4},{9,5},... | collective-permute-start | bytes 98312 | tf_op jit(solution)/shard_map/ppermute | solution.py:414
  9.4 0.2 collective-permute-start.1
  9.6 0.0 copy-done.1
  9.6 0.0 copy-start.2
  9.6 0.8 %copy-done.2 = f32[16,3,3,3,3]{0,4,3,2,1:T(4,128)S(1)} copy-done((f32[16,3,3,3,3]{0,4,3,2,1:T(4,128)S(1)}, f32[16,3,3,3,3]{0,4,3,2,1:T(4,128)}, u32[]{:S(2)}) %copy-start.2) | copy-done | bytes 5208
  10.4 0.0 copy-start
  10.4 0.7 %prepare.1 = (bf16[320,240]{1,0:T(8,128)(2,1)S(1)}, bf16[288,640]{1,0:T(8,128)(2,1)S(1)}) custom-call(f32[3,3,3,3,16]{4,3,2,1,0:T(4,128)S(1)} %bitcast.3, f32[3,3,3,3,16]{4,3,2,1,0:T(4,128)S(1)} %bitcast.4, bf16[16,1024]{1,0:T(8,128)(2,1)S(1)} %get-tuple-element.15.gate_ref), custom_call_target="tpu_custom_call" | custom-call | flops 1000000000 | bytes 1000000 | tf_op jit(solution)/shard_map/prepare/pallas_call | solution.py:455
  11.1 0.4 copy-done
  11.5 0.2 target.1.target_ref
  11.7 1.6 %collective-permute-done.1 = bf16[16,1024]{1,0:T(8,128)(2,1)S(1)} collective-permute-done((bf16[16,1024]{1,0:T(8,128)(2,1)S(1)}, bf16[16,1024]{1,0:T(8,128)(2,1)S(1)}, u32[]{:S(2)}, u32[]{:S(2)}) %collective-permute-start.1) | collective-permute-done | bytes 32800 | tf_op jit(solution)/shard_map/ppermute | solution.py:414
  13.3 0.4 %collective-permute-done.2 = bf16[16,1024]{1,0:T(8,128)(2,1)S(1)} collective-permute-done((bf16[16,1024]{1,0:T(8,128)(2,1)S(1)}, bf16[16,1024]{1,0:T(8,128)(2,1)S(1)}, u32[]{:S(2)}, u32[]{:S(2)}) %collective-permute-start.2) | collective-permute-done | bytes 32800 | tf_op jit(solution)/shard_map/ppermute | solution.py:414
  13.7 0.0 collective-permute-done.3
  13.7 0.1 collective-permute-start.4
  13.8 1.3 %collective-permute-done.4.far_ref = bf16[64,1024]{1,0:T(8,128)(2,1)S(1)} collective-permute-done((bf16[64,1024]{1,0:T(8,128)(2,1)S(1)}, bf16[64,1024]{1,0:T(8,128)(2,1)S(1)}, u32[]{:S(2)}, u32[]{:S(2)}) %collective-permute-start.4) | collective-permute-done | bytes 131104 | tf_op jit(solution)/shard_map/ppermute | solution.py:485
  15.2 0.4 %match.1 = f32[16,32,128]{2,1,0:T(8,128)S(1)} custom-call(bf16[64,1024]{1,0:T(8,128)(2,1)S(1)} %constant_dynamic-update-slice_fusion.2.near_ref, bf16[64,1024]{1,0:T(8,128)(2,1)S(1)} %collective-permute-done.4.far_ref, bf16[256,1024]{1,0:T(8,128)(2,1)S(1)} %target.1.target_ref), custom_call_target="tpu_custom_call" | custom-call | tf_op jit(solution)/shard_map/match/pallas_call | solution.py:486
  15.6 12.1 %all_to_all.10 = f16[16,32,128]{2,1,0:T(8,128)(2,1)S(1)} all-to-all(f16[16,32,128]{2,1,0:T(8,128)(2,1)S(1)} %convert_element_type.12), channel_id=1, replica_groups=mesh['pairs'=2,'tgt'=16] {'tgt'}, dimensions={0} | all-to-all | bytes 262144 | tf_op jit(solution)/shard_map/all_to_all | solution.py:423
  27.8 3.2 %consensus.1 = f32[16,24,128]{2,1,0:T(8,128)S(1)} custom-call(f32[16,32,128]{2,1,0:T(8,128)S(1)} %convert_element_type.13.came_ref, bf16[320,240]{1,0:T(8,128)(2,1)S(1)} %get-tuple-element.13.gate_ref.first_ref, bf16[288,640]{1,0:T(8,128)(2,1)S(1)} %get-tuple-element.14.second_ref), custom_call_target="tpu_custom_call" | custom-call | tf_op jit(solution)/shard_map/consensus/pallas_call | solution.py:505
  30.9 10.0 %all_to_all.11 = f16[16,24,128]{2,1,0:T(8,128)(2,1)S(1)} all-to-all(f16[16,24,128]{2,1,0:T(8,128)(2,1)S(1)} %convert_element_type.14), channel_id=1, replica_groups=mesh['pairs'=2,'tgt'=16] {'tgt'}, dimensions={0} | all-to-all | bytes 196608 | tf_op jit(solution)/shard_map/all_to_all | solution.py:423
  40.9 0.9 %finish.1 = f32[128,2,128]{2,1,0:T(2,128)} custom-call(f32[16,24,128]{2,1,0:T(8,128)S(1)} %convert_element_type.15.came_ref), custom_call_target="tpu_custom_call" | custom-call | tf_op jit(solution)/shard_map/finish/pallas_call | solution.py:515
  (8 shorter events, 0.1 us)
Async XLA Ops:
  0.0 9.6 %copy-start.1 = (f32[16,3,3,3,3]{0,4,3,2,1:T(4,128)S(1)}, f32[16,3,3,3,3]{0,4,3,2,1:T(4,128)}, u32[]{:S(2)}) copy-start(f32[16,3,3,3,3]{0,4,3,2,1:T(4,128)} %param.6) | copy-start | bytes 15556
  0.0 4.9 %collective-permute-start = (bf16[8,1024]{1,0:T(8,128)(2,1)}, bf16[8,1024]{1,0:T(8,128)(2,1)S(1)}, u32[]{:S(2)}, u32[]{:S(2)}) collective-permute-start(bf16[8,1024]{1,0:T(8,128)(2,1)} %param.4), channel_id=1, source_target_pairs={{0,2},{1,3},{2,0},{3,1},{4,6},{5,7},{6,4},{7,5},{8,10},{9,11},{10,... | collective-permute-start | bytes 49160 | tf_op jit(solution)/shard_map/ppermute | solution.py:414
  4.9 8.8 %collective-permute-start.3 = (bf16[16,1024]{1,0:T(8,128)(2,1)S(1)}, bf16[16,1024]{1,0:T(8,128)(2,1)S(1)}, u32[]{:S(2)}, u32[]{:S(2)}) collective-permute-start(bf16[16,1024]{1,0:T(8,128)(2,1)S(1)} %get-tuple-element.15.gate_ref), channel_id=1, source_target_pairs={{0,8},{1,9},{2,10},{3,11},{4,12},{5,13},{6,14},{7,15},{8,0},{9,1},... | collective-permute-start | bytes 98312 | tf_op jit(solution)/shard_map/ppermute | solution.py:414
  8.0 5.7 %collective-permute-start.2 = (bf16[16,1024]{1,0:T(8,128)(2,1)S(1)}, bf16[16,1024]{1,0:T(8,128)(2,1)S(1)}, u32[]{:S(2)}, u32[]{:S(2)}) collective-permute-start(bf16[16,1024]{1,0:T(8,128)(2,1)S(1)} %get-tuple-element.15.gate_ref), channel_id=1, source_target_pairs={{0,12},{1,13},{2,14},{3,15},{4,8},{5,9},{6,10},{7,11},{8,4},{9,5},... | collective-permute-start | bytes 98312 | tf_op jit(solution)/shard_map/ppermute | solution.py:414
  9.4 3.9 %collective-permute-start.1 = (bf16[16,1024]{1,0:T(8,128)(2,1)S(1)}, bf16[16,1024]{1,0:T(8,128)(2,1)S(1)}, u32[]{:S(2)}, u32[]{:S(2)}) collective-permute-start(bf16[16,1024]{1,0:T(8,128)(2,1)S(1)} %get-tuple-element.15.gate_ref), channel_id=1, source_target_pairs={{0,4},{1,5},{2,6},{3,7},{4,0},{5,1},{6,2},{7,3},{8,12},{9,13},{10,... | collective-permute-start | bytes 98312 | tf_op jit(solution)/shard_map/ppermute | solution.py:414
  9.6 0.8 %copy-start.2 = (f32[16,3,3,3,3]{0,4,3,2,1:T(4,128)S(1)}, f32[16,3,3,3,3]{0,4,3,2,1:T(4,128)}, u32[]{:S(2)}) copy-start(f32[16,3,3,3,3]{0,4,3,2,1:T(4,128)} %param.7) | copy-start | bytes 15556
  10.4 1.0 %copy-start = (bf16[2,128,1024]{2,1,0:T(8,128)(2,1)S(1)}, bf16[2,128,1024]{2,1,0:T(8,128)(2,1)}, u32[]{:S(2)}) copy-start(bf16[2,128,1024]{2,1,0:T(8,128)(2,1)} %target_ref.1) | copy-start | bytes 1572868
  13.7 1.4 %collective-permute-start.4 = (bf16[64,1024]{1,0:T(8,128)(2,1)S(1)}, bf16[64,1024]{1,0:T(8,128)(2,1)S(1)}, u32[]{:S(2)}, u32[]{:S(2)}) collective-permute-start(bf16[64,1024]{1,0:T(8,128)(2,1)S(1)} %constant_dynamic-update-slice_fusion.2.near_ref), channel_id=1, source_target_pairs={{0,1},{1,0},{2,3},{3,2},{4,5},{5,4},{6,7},{7,6},{8,9},{9,8},{10,11... | collective-permute-start | bytes 393224 | tf_op jit(solution)/shard_map/ppermute | solution.py:485

commit v8 on v7

--- a/solution.py
+++ b/solution.py
@@ -138,29 +138,35 @@
         unit_ref[row * columns : (row + 1) * columns] = unit(target_ref[row])
 
 
-def match_kernel(
-    local, masks, near_ref, far_ref, target_ref, send_ref, source_ref, order_ref
-):
+def correlate(source, target):
+    return lax.dot_general(
+        unit(source), target, (((1,), (1,)), ((), ())), preferred_element_type=F32
+    )
+
+
+def near_kernel(near_ref, target_ref, out_ref):
+    out_ref[...] = correlate(near_ref[...], target_ref[...])
+
+
+def match_kernel(local, masks, near_ref, far_ref, target_ref, send_ref, order_ref):
     rows, padded, columns = order_ref.shape
     cells = padded - 2 * SUBLANES
-    middle = near_ref.shape[0]
-    source_ref[:middle] = unit(near_ref[...])
-    source_ref[middle:] = unit(far_ref[...])
-    correlation = lax.dot_general(
-        source_ref[...], target_ref[...], (((1,), (1,)), ((), ())), preferred_element_type=F32
-    )
+    far = correlate(far_ref[...], target_ref[...])
     position = lax.axis_index("tgt")
     window = max(SUBLANES, local + 4)
     blank = jnp.zeros((SUBLANES, columns), F32)
     for row in range(rows):
         order_ref[row, :SUBLANES, :] = blank
         order_ref[row, SUBLANES + cells :, :] = blank
+        lanes = slice(row * columns, (row + 1) * columns)
+        middle = len(masks) // 2
         for piece, mask in enumerate(masks):
             start = SUBLANES + (position ^ mask) * local
             if local % SUBLANES == 0:
                 start = pl.multiple_of(start, SUBLANES)
-            order_ref[row, pl.ds(start, local), :] = correlation[
-                piece * local : (piece + 1) * local, row * columns : (row + 1) * columns
+            held, first = (near_ref, piece) if piece < middle else (far, piece - middle)
+            order_ref[row, pl.ds(start, local), :] = held[
+                first * local : (first + 1) * local, lanes
             ]
         source_best = jnp.max(order_ref[row], axis=0, keepdims=True)
         scale = 1.0 / jnp.maximum(source_best, TINY)
@@ -483,13 +489,21 @@
         (near, target_unit, first_weights)
     )
     far = lax.ppermute(near, "tgt", [(i, i ^ 1) for i in range(devices)])
+    near = pl.pallas_call(
+        near_kernel,
+        out_shape=jax.ShapeDtypeStruct((cells // 2, rows * columns), F32),
+        in_specs=[VMEM] * 2,
+        out_specs=VMEM,
+        cost_estimate=pl.CostEstimate(flops=10**8, bytes_accessed=10**6, transcendentals=0),
+        compiler_params=room(),
+        name="near",
+    )(near, target_unit)
     slots = pl.pallas_call(
         functools.partial(match_kernel, local, masks),
         out_shape=jax.ShapeDtypeStruct((devices, whole_tiles(rows * (window + 2)), columns), F32),
         in_specs=[VMEM] * 3,
         out_specs=VMEM,
         scratch_shapes=[
-            pltpu.VMEM((cells, channels), BF16),
             pltpu.VMEM((rows, cells + 2 * SUBLANES, columns), F32),
         ],
         compiler_params=room(),

time: 42.1 us -> 42.1 us (level)
  transfers between devices with their start and end apart: 5 -> 5, of which waited for: 4 -> 4; matrix products, arithmetic and copies ran while one was open for 2% -> 2% of each run, Pallas kernels for 2% -> 3%
where the time goes in v8:
time: 42.1 us; the launch traced here: 41.7 us
  blocking collectives  22.1 us (52%)
  starting transfers between devices  7.74 us (18%)
  Pallas kernels  5.63 us (13%)
  waiting for transfers between devices  4.21 us (10%)
  local copies, waits for them, and re-layouts  1.95 us (5%)
    all_to_all x2, blocking collectives, exchange(): return lax.all_to_all(slots, 'tgt', 0, 0, tiled=True)  22.1 us
    ppermute x4, starting transfers between devices, gather_sources(): lax.ppermute(value, 'tgt', [(i, i ^ mask) for i in range(devices)])  7.67 us
    ppermute x4, waiting for transfers between devices, gather_sources(): lax.ppermute(value, 'tgt', [(i, i ^ mask) for i in range(devices)])  3.2 us
    pallas_call x1, Pallas kernels, shards(): pl.pallas_call(functools.partial(consensus_kernel, parts, local, rows), o...  3.16 us
    unnamed x9, local copies, waits for them, and re-layouts  1.95 us
    ppermute x1, waiting for transfers between devices, shards(): far = lax.ppermute(near, 'tgt', [(i, i ^ 1) for i in range(devices)])  1.01 us
    pallas_call x1, Pallas kernels, shards(): pl.pallas_call(functools.partial(finish_kernel, local), out_shape=jax.Sha...  0.86 us
  transfers between devices with their start and end apart: 5, of which 4 were waited for; matrix products, arithmetic and copies ran while one was open for 2% of the time, Pallas kernels for 3%

profile of v8, /device:TPU:0, one launch (start us, length us, event | category | flops | bytes accessed | tf_op | source)
XLA Modules:
  0.0 41.7 jit_solution(17386247769201966867)
XLA Ops:
  0.0 0.0 copy-start.1
  0.0 3.0 %collective-permute-start = (bf16[8,1024]{1,0:T(8,128)(2,1)}, bf16[8,1024]{1,0:T(8,128)(2,1)S(1)}, u32[]{:S(2)}, u32[]{:S(2)}) collective-permute-start(bf16[8,1024]{1,0:T(8,128)(2,1)} %param.4), channel_id=1, source_target_pairs={{0,2},{1,3},{2,0},{3,1},{4,6},{5,7},{6,4},{7,5},{8,10},{9,11},{10,... | collective-permute-start | bytes 49160 | tf_op jit(solution)/shard_map/ppermute | solution.py:420
  3.0 0.8 %constant_dynamic-update-slice_fusion.1 = (bf16[16,1024]{1,0:T(8,128)(2,1)S(1)}, bf16[64,1024]{1,0:T(8,128)(2,1)S(1)}) fusion(bf16[8,1024]{1,0:T(8,128)(2,1)} %param.4), kind=kLoop, calls=%fused_computation.1 | loop fusion | bytes 49152
  3.8 1.2 %collective-permute-done = bf16[8,1024]{1,0:T(8,128)(2,1)S(1)} collective-permute-done((bf16[8,1024]{1,0:T(8,128)(2,1)}, bf16[8,1024]{1,0:T(8,128)(2,1)S(1)}, u32[]{:S(2)}, u32[]{:S(2)}) %collective-permute-start) | collective-permute-done | bytes 16416 | tf_op jit(solution)/shard_map/ppermute | solution.py:420
  4.9 3.1 %collective-permute-start.3 = (bf16[16,1024]{1,0:T(8,128)(2,1)S(1)}, bf16[16,1024]{1,0:T(8,128)(2,1)S(1)}, u32[]{:S(2)}, u32[]{:S(2)}) collective-permute-start(bf16[16,1024]{1,0:T(8,128)(2,1)S(1)} %get-tuple-element.15.gate_ref), channel_id=1, source_target_pairs={{0,8},{1,9},{2,10},{3,11},{4,12},{5,13},{6,14},{7,15},{8,0},{9,1},... | collective-permute-start | bytes 98312 | tf_op jit(solution)/shard_map/ppermute | solution.py:420
  8.0 1.3 %collective-permute-start.2 = (bf16[16,1024]{1,0:T(8,128)(2,1)S(1)}, bf16[16,1024]{1,0:T(8,128)(2,1)S(1)}, u32[]{:S(2)}, u32[]{:S(2)}) collective-permute-start(bf16[16,1024]{1,0:T(8,128)(2,1)S(1)} %get-tuple-element.15.gate_ref), channel_id=1, source_target_pairs={{0,12},{1,13},{2,14},{3,15},{4,8},{5,9},{6,10},{7,11},{8,4},{9,5},... | collective-permute-start | bytes 98312 | tf_op jit(solution)/shard_map/ppermute | solution.py:420
  9.4 0.2 collective-permute-start.1
  9.6 0.0 copy-done.1
  9.6 0.0 copy-start.2
  9.6 0.8 %copy-done.2 = f32[16,3,3,3,3]{0,4,3,2,1:T(4,128)S(1)} copy-done((f32[16,3,3,3,3]{0,4,3,2,1:T(4,128)S(1)}, f32[16,3,3,3,3]{0,4,3,2,1:T(4,128)}, u32[]{:S(2)}) %copy-start.2) | copy-done | bytes 5208
  10.4 0.7 %prepare.1 = (bf16[320,240]{1,0:T(8,128)(2,1)S(1)}, bf16[288,640]{1,0:T(8,128)(2,1)S(1)}) custom-call(f32[3,3,3,3,16]{4,3,2,1,0:T(4,128)S(1)} %bitcast.3, f32[3,3,3,3,16]{4,3,2,1,0:T(4,128)S(1)} %bitcast.4, bf16[16,1024]{1,0:T(8,128)(2,1)S(1)} %get-tuple-element.15.gate_ref), custom_call_target="tpu_custom_call" | custom-call | flops 1000000000 | bytes 1000000 | tf_op jit(solution)/shard_map/prepare/pallas_call | solution.py:461
  11.1 0.4 copy-done
  11.5 0.2 target.1.target_ref
  11.7 1.6 %collective-permute-done.1 = bf16[16,1024]{1,0:T(8,128)(2,1)S(1)} collective-permute-done((bf16[16,1024]{1,0:T(8,128)(2,1)S(1)}, bf16[16,1024]{1,0:T(8,128)(2,1)S(1)}, u32[]{:S(2)}, u32[]{:S(2)}) %collective-permute-start.1) | collective-permute-done | bytes 32800 | tf_op jit(solution)/shard_map/ppermute | solution.py:420
  13.3 0.4 %collective-permute-done.2 = bf16[16,1024]{1,0:T(8,128)(2,1)S(1)} collective-permute-done((bf16[16,1024]{1,0:T(8,128)(2,1)S(1)}, bf16[16,1024]{1,0:T(8,128)(2,1)S(1)}, u32[]{:S(2)}, u32[]{:S(2)}) %collective-permute-start.2) | collective-permute-done | bytes 32800 | tf_op jit(solution)/shard_map/ppermute | solution.py:420
  13.7 0.0 collective-permute-done.3
  13.7 0.1 collective-permute-start.4
  13.8 0.3 near.1.near_ref
  14.1 1.0 %collective-permute-done.4.far_ref = bf16[64,1024]{1,0:T(8,128)(2,1)S(1)} collective-permute-done((bf16[64,1024]{1,0:T(8,128)(2,1)S(1)}, bf16[64,1024]{1,0:T(8,128)(2,1)S(1)}, u32[]{:S(2)}, u32[]{:S(2)}) %collective-permute-start.4) | collective-permute-done | bytes 131104 | tf_op jit(solution)/shard_map/ppermute | solution.py:491
  15.2 0.4 match.1
  15.6 12.1 %all_to_all.10 = f16[16,32,128]{2,1,0:T(8,128)(2,1)S(1)} all-to-all(f16[16,32,128]{2,1,0:T(8,128)(2,1)S(1)} %convert_element_type.12), channel_id=1, replica_groups=mesh['pairs'=2,'tgt'=16] {'tgt'}, dimensions={0} | all-to-all | bytes 262144 | tf_op jit(solution)/shard_map/all_to_all | solution.py:429
  27.7 3.2 %consensus.1 = f32[16,24,128]{2,1,0:T(8,128)S(1)} custom-call(f32[16,32,128]{2,1,0:T(8,128)S(1)} %convert_element_type.13.came_ref, bf16[320,240]{1,0:T(8,128)(2,1)S(1)} %get-tuple-element.13.gate_ref.first_ref, bf16[288,640]{1,0:T(8,128)(2,1)S(1)} %get-tuple-element.14.second_ref), custom_call_target="tpu_custom_call" | custom-call | tf_op jit(solution)/shard_map/consensus/pallas_call | solution.py:519
  30.9 10.0 %all_to_all.11 = f16[16,24,128]{2,1,0:T(8,128)(2,1)S(1)} all-to-all(f16[16,24,128]{2,1,0:T(8,128)(2,1)S(1)} %convert_element_type.14), channel_id=1, replica_groups=mesh['pairs'=2,'tgt'=16] {'tgt'}, dimensions={0} | all-to-all | bytes 196608 | tf_op jit(solution)/shard_map/all_to_all | solution.py:429
  40.9 0.9 %finish.1 = f32[128,2,128]{2,1,0:T(2,128)} custom-call(f32[16,24,128]{2,1,0:T(8,128)S(1)} %convert_element_type.15.came_ref), custom_call_target="tpu_custom_call" | custom-call | tf_op jit(solution)/shard_map/finish/pallas_call | solution.py:529
  (9 shorter events, 0.1 us)
Async XLA Ops:
  0.0 9.6 %copy-start.1 = (f32[16,3,3,3,3]{0,4,3,2,1:T(4,128)S(1)}, f32[16,3,3,3,3]{0,4,3,2,1:T(4,128)}, u32[]{:S(2)}) copy-start(f32[16,3,3,3,3]{0,4,3,2,1:T(4,128)} %param.6) | copy-start | bytes 15556
  0.0 4.9 %collective-permute-start = (bf16[8,1024]{1,0:T(8,128)(2,1)}, bf16[8,1024]{1,0:T(8,128)(2,1)S(1)}, u32[]{:S(2)}, u32[]{:S(2)}) collective-permute-start(bf16[8,1024]{1,0:T(8,128)(2,1)} %param.4), channel_id=1, source_target_pairs={{0,2},{1,3},{2,0},{3,1},{4,6},{5,7},{6,4},{7,5},{8,10},{9,11},{10,... | collective-permute-start | bytes 49160 | tf_op jit(solution)/shard_map/ppermute | solution.py:420
  4.9 8.8 %collective-permute-start.3 = (bf16[16,1024]{1,0:T(8,128)(2,1)S(1)}, bf16[16,1024]{1,0:T(8,128)(2,1)S(1)}, u32[]{:S(2)}, u32[]{:S(2)}) collective-permute-start(bf16[16,1024]{1,0:T(8,128)(2,1)S(1)} %get-tuple-element.15.gate_ref), channel_id=1, source_target_pairs={{0,8},{1,9},{2,10},{3,11},{4,12},{5,13},{6,14},{7,15},{8,0},{9,1},... | collective-permute-start | bytes 98312 | tf_op jit(solution)/shard_map/ppermute | solution.py:420
  8.0 5.7 %collective-permute-start.2 = (bf16[16,1024]{1,0:T(8,128)(2,1)S(1)}, bf16[16,1024]{1,0:T(8,128)(2,1)S(1)}, u32[]{:S(2)}, u32[]{:S(2)}) collective-permute-start(bf16[16,1024]{1,0:T(8,128)(2,1)S(1)} %get-tuple-element.15.gate_ref), channel_id=1, source_target_pairs={{0,12},{1,13},{2,14},{3,15},{4,8},{5,9},{6,10},{7,11},{8,4},{9,5},... | collective-permute-start | bytes 98312 | tf_op jit(solution)/shard_map/ppermute | solution.py:420
  9.4 3.9 %collective-permute-start.1 = (bf16[16,1024]{1,0:T(8,128)(2,1)S(1)}, bf16[16,1024]{1,0:T(8,128)(2,1)S(1)}, u32[]{:S(2)}, u32[]{:S(2)}) collective-permute-start(bf16[16,1024]{1,0:T(8,128)(2,1)S(1)} %get-tuple-element.15.gate_ref), channel_id=1, source_target_pairs={{0,4},{1,5},{2,6},{3,7},{4,0},{5,1},{6,2},{7,3},{8,12},{9,13},{10,... | collective-permute-start | bytes 98312 | tf_op jit(solution)/shard_map/ppermute | solution.py:420
  9.6 0.8 %copy-start.2 = (f32[16,3,3,3,3]{0,4,3,2,1:T(4,128)S(1)}, f32[16,3,3,3,3]{0,4,3,2,1:T(4,128)}, u32[]{:S(2)}) copy-start(f32[16,3,3,3,3]{0,4,3,2,1:T(4,128)} %param.7) | copy-start | bytes 15556
  10.4 1.0 %copy-start = (bf16[2,128,1024]{2,1,0:T(8,128)(2,1)S(1)}, bf16[2,128,1024]{2,1,0:T(8,128)(2,1)}, u32[]{:S(2)}) copy-start(bf16[2,128,1024]{2,1,0:T(8,128)(2,1)} %target_ref.1) | copy-start | bytes 1572868
  13.7 1.4 %collective-permute-start.4 = (bf16[64,1024]{1,0:T(8,128)(2,1)S(1)}, bf16[64,1024]{1,0:T(8,128)(2,1)S(1)}, u32[]{:S(2)}, u32[]{:S(2)}) collective-permute-start(bf16[64,1024]{1,0:T(8,128)(2,1)S(1)} %constant_dynamic-update-slice_fusion.2.near_ref), channel_id=1, source_target_pairs={{0,1},{1,0},{2,3},{3,2},{4,5},{5,4},{6,7},{7,6},{8,9},{9,8},{10,11... | collective-permute-start | bytes 393224 | tf_op jit(solution)/shard_map/ppermute | solution.py:491

commit v9 on v8

--- a/solution.py
+++ b/solution.py
@@ -244,7 +244,7 @@
                 best[number] = jnp.maximum(best[number], block[first : first + SUBLANES])
         return tuple(best)
 
-    best = lax.fori_loop(0, devices, survey, (zero,) * len(parts), unroll=4)
+    best = lax.fori_loop(0, devices, survey, (zero,) * len(parts), unroll=min(16, devices))
     scales = [
         jnp.broadcast_to(1.0 / (jnp.max(most, axis=1, keepdims=True) + EPSILON), most.shape)
         for most in best

time: 42.1 us -> 42 us (level)
  no operation moved by 1% of the time
where the time goes in v9:
time: 42 us; the launch traced here: 41.7 us
  blocking collectives  22.1 us (53%)
  starting transfers between devices  7.74 us (18%)
  Pallas kernels  5.6 us (13%)
  waiting for transfers between devices  4.21 us (10%)
  local copies, waits for them, and re-layouts  1.95 us (5%)
    all_to_all x2, blocking collectives, exchange(): return lax.all_to_all(slots, 'tgt', 0, 0, tiled=True)  22.1 us
    ppermute x4, starting transfers between devices, gather_sources(): lax.ppermute(value, 'tgt', [(i, i ^ mask) for i in range(devices)])  7.67 us
    ppermute x4, waiting for transfers between devices, gather_sources(): lax.ppermute(value, 'tgt', [(i, i ^ mask) for i in range(devices)])  3.2 us
    pallas_call x1, Pallas kernels, shards(): pl.pallas_call(functools.partial(consensus_kernel, parts, local, rows), o...  3.13 us
    unnamed x9, local copies, waits for them, and re-layouts  1.95 us
    ppermute x1, waiting for transfers between devices, shards(): far = lax.ppermute(near, 'tgt', [(i, i ^ 1) for i in range(devices)])  1.01 us
    pallas_call x1, Pallas kernels, shards(): pl.pallas_call(functools.partial(finish_kernel, local), out_shape=jax.Sha...  0.86 us
  transfers between devices with their start and end apart: 5, of which 4 were waited for; matrix products, arithmetic and copies ran while one was open for 2% of the time, Pallas kernels for 3%

profile of v9, /device:TPU:0, one launch (start us, length us, event | category | flops | bytes accessed | tf_op | source)
XLA Modules:
  0.0 41.7 jit_solution(4496850259174412322)
XLA Ops:
  0.0 0.0 copy-start.1
  0.0 3.0 %collective-permute-start = (bf16[8,1024]{1,0:T(8,128)(2,1)}, bf16[8,1024]{1,0:T(8,128)(2,1)S(1)}, u32[]{:S(2)}, u32[]{:S(2)}) collective-permute-start(bf16[8,1024]{1,0:T(8,128)(2,1)} %param.4), channel_id=1, source_target_pairs={{0,2},{1,3},{2,0},{3,1},{4,6},{5,7},{6,4},{7,5},{8,10},{9,11},{10,... | collective-permute-start | bytes 49160 | tf_op jit(solution)/shard_map/ppermute | solution.py:420
  3.0 0.8 %constant_dynamic-update-slice_fusion.1 = (bf16[16,1024]{1,0:T(8,128)(2,1)S(1)}, bf16[64,1024]{1,0:T(8,128)(2,1)S(1)}) fusion(bf16[8,1024]{1,0:T(8,128)(2,1)} %param.4), kind=kLoop, calls=%fused_computation.1 | loop fusion | bytes 49152
  3.8 1.2 %collective-permute-done = bf16[8,1024]{1,0:T(8,128)(2,1)S(1)} collective-permute-done((bf16[8,1024]{1,0:T(8,128)(2,1)}, bf16[8,1024]{1,0:T(8,128)(2,1)S(1)}, u32[]{:S(2)}, u32[]{:S(2)}) %collective-permute-start) | collective-permute-done | bytes 16416 | tf_op jit(solution)/shard_map/ppermute | solution.py:420
  4.9 3.1 %collective-permute-start.3 = (bf16[16,1024]{1,0:T(8,128)(2,1)S(1)}, bf16[16,1024]{1,0:T(8,128)(2,1)S(1)}, u32[]{:S(2)}, u32[]{:S(2)}) collective-permute-start(bf16[16,1024]{1,0:T(8,128)(2,1)S(1)} %get-tuple-element.15.gate_ref), channel_id=1, source_target_pairs={{0,8},{1,9},{2,10},{3,11},{4,12},{5,13},{6,14},{7,15},{8,0},{9,1},... | collective-permute-start | bytes 98312 | tf_op jit(solution)/shard_map/ppermute | solution.py:420
  8.0 1.3 %collective-permute-start.2 = (bf16[16,1024]{1,0:T(8,128)(2,1)S(1)}, bf16[16,1024]{1,0:T(8,128)(2,1)S(1)}, u32[]{:S(2)}, u32[]{:S(2)}) collective-permute-start(bf16[16,1024]{1,0:T(8,128)(2,1)S(1)} %get-tuple-element.15.gate_ref), channel_id=1, source_target_pairs={{0,12},{1,13},{2,14},{3,15},{4,8},{5,9},{6,10},{7,11},{8,4},{9,5},... | collective-permute-start | bytes 98312 | tf_op jit(solution)/shard_map/ppermute | solution.py:420
  9.4 0.2 collective-permute-start.1
  9.6 0.0 copy-done.1
  9.6 0.0 copy-start.2
  9.6 0.8 %copy-done.2 = f32[16,3,3,3,3]{0,4,3,2,1:T(4,128)S(1)} copy-done((f32[16,3,3,3,3]{0,4,3,2,1:T(4,128)S(1)}, f32[16,3,3,3,3]{0,4,3,2,1:T(4,128)}, u32[]{:S(2)}) %copy-start.2) | copy-done | bytes 5208
  10.4 0.7 %prepare.1 = (bf16[320,240]{1,0:T(8,128)(2,1)S(1)}, bf16[288,640]{1,0:T(8,128)(2,1)S(1)}) custom-call(f32[3,3,3,3,16]{4,3,2,1,0:T(4,128)S(1)} %bitcast.3, f32[3,3,3,3,16]{4,3,2,1,0:T(4,128)S(1)} %bitcast.4, bf16[16,1024]{1,0:T(8,128)(2,1)S(1)} %get-tuple-element.15.gate_ref), custom_call_target="tpu_custom_call" | custom-call | flops 1000000000 | bytes 1000000 | tf_op jit(solution)/shard_map/prepare/pallas_call | solution.py:461
  11.1 0.4 copy-done
  11.5 0.2 target.1.target_ref
  11.7 1.6 %collective-permute-done.1 = bf16[16,1024]{1,0:T(8,128)(2,1)S(1)} collective-permute-done((bf16[16,1024]{1,0:T(8,128)(2,1)S(1)}, bf16[16,1024]{1,0:T(8,128)(2,1)S(1)}, u32[]{:S(2)}, u32[]{:S(2)}) %collective-permute-start.1) | collective-permute-done | bytes 32800 | tf_op jit(solution)/shard_map/ppermute | solution.py:420
  13.3 0.4 %collective-permute-done.2 = bf16[16,1024]{1,0:T(8,128)(2,1)S(1)} collective-permute-done((bf16[16,1024]{1,0:T(8,128)(2,1)S(1)}, bf16[16,1024]{1,0:T(8,128)(2,1)S(1)}, u32[]{:S(2)}, u32[]{:S(2)}) %collective-permute-start.2) | collective-permute-done | bytes 32800 | tf_op jit(solution)/shard_map/ppermute | solution.py:420
  13.7 0.0 collective-permute-done.3
  13.7 0.1 collective-permute-start.4
  13.8 0.3 near.1.near_ref
  14.1 1.0 %collective-permute-done.4.far_ref = bf16[64,1024]{1,0:T(8,128)(2,1)S(1)} collective-permute-done((bf16[64,1024]{1,0:T(8,128)(2,1)S(1)}, bf16[64,1024]{1,0:T(8,128)(2,1)S(1)}, u32[]{:S(2)}, u32[]{:S(2)}) %collective-permute-start.4) | collective-permute-done | bytes 131104 | tf_op jit(solution)/shard_map/ppermute | solution.py:491
  15.2 0.4 match.1
  15.6 12.1 %all_to_all.10 = f16[16,32,128]{2,1,0:T(8,128)(2,1)S(1)} all-to-all(f16[16,32,128]{2,1,0:T(8,128)(2,1)S(1)} %convert_element_type.12), channel_id=1, replica_groups=mesh['pairs'=2,'tgt'=16] {'tgt'}, dimensions={0} | all-to-all | bytes 262144 | tf_op jit(solution)/shard_map/all_to_all | solution.py:429
  27.7 3.1 %consensus.1 = f32[16,24,128]{2,1,0:T(8,128)S(1)} custom-call(f32[16,32,128]{2,1,0:T(8,128)S(1)} %convert_element_type.13.came_ref, bf16[320,240]{1,0:T(8,128)(2,1)S(1)} %get-tuple-element.13.gate_ref.first_ref, bf16[288,640]{1,0:T(8,128)(2,1)S(1)} %get-tuple-element.14.second_ref), custom_call_target="tpu_custom_call" | custom-call | tf_op jit(solution)/shard_map/consensus/pallas_call | solution.py:519
  30.9 10.0 %all_to_all.11 = f16[16,24,128]{2,1,0:T(8,128)(2,1)S(1)} all-to-all(f16[16,24,128]{2,1,0:T(8,128)(2,1)S(1)} %convert_element_type.14), channel_id=1, replica_groups=mesh['pairs'=2,'tgt'=16] {'tgt'}, dimensions={0} | all-to-all | bytes 196608 | tf_op jit(solution)/shard_map/all_to_all | solution.py:429
  40.9 0.9 %finish.1 = f32[128,2,128]{2,1,0:T(2,128)} custom-call(f32[16,24,128]{2,1,0:T(8,128)S(1)} %convert_element_type.15.came_ref), custom_call_target="tpu_custom_call" | custom-call | tf_op jit(solution)/shard_map/finish/pallas_call | solution.py:529
  (9 shorter events, 0.1 us)
Async XLA Ops:
  0.0 9.6 %copy-start.1 = (f32[16,3,3,3,3]{0,4,3,2,1:T(4,128)S(1)}, f32[16,3,3,3,3]{0,4,3,2,1:T(4,128)}, u32[]{:S(2)}) copy-start(f32[16,3,3,3,3]{0,4,3,2,1:T(4,128)} %param.6) | copy-start | bytes 15556
  0.0 4.9 %collective-permute-start = (bf16[8,1024]{1,0:T(8,128)(2,1)}, bf16[8,1024]{1,0:T(8,128)(2,1)S(1)}, u32[]{:S(2)}, u32[]{:S(2)}) collective-permute-start(bf16[8,1024]{1,0:T(8,128)(2,1)} %param.4), channel_id=1, source_target_pairs={{0,2},{1,3},{2,0},{3,1},{4,6},{5,7},{6,4},{7,5},{8,10},{9,11},{10,... | collective-permute-start | bytes 49160 | tf_op jit(solution)/shard_map/ppermute | solution.py:420
  4.9 8.8 %collective-permute-start.3 = (bf16[16,1024]{1,0:T(8,128)(2,1)S(1)}, bf16[16,1024]{1,0:T(8,128)(2,1)S(1)}, u32[]{:S(2)}, u32[]{:S(2)}) collective-permute-start(bf16[16,1024]{1,0:T(8,128)(2,1)S(1)} %get-tuple-element.15.gate_ref), channel_id=1, source_target_pairs={{0,8},{1,9},{2,10},{3,11},{4,12},{5,13},{6,14},{7,15},{8,0},{9,1},... | collective-permute-start | bytes 98312 | tf_op jit(solution)/shard_map/ppermute | solution.py:420
  8.0 5.7 %collective-permute-start.2 = (bf16[16,1024]{1,0:T(8,128)(2,1)S(1)}, bf16[16,1024]{1,0:T(8,128)(2,1)S(1)}, u32[]{:S(2)}, u32[]{:S(2)}) collective-permute-start(bf16[16,1024]{1,0:T(8,128)(2,1)S(1)} %get-tuple-element.15.gate_ref), channel_id=1, source_target_pairs={{0,12},{1,13},{2,14},{3,15},{4,8},{5,9},{6,10},{7,11},{8,4},{9,5},... | collective-permute-start | bytes 98312 | tf_op jit(solution)/shard_map/ppermute | solution.py:420
  9.4 3.9 %collective-permute-start.1 = (bf16[16,1024]{1,0:T(8,128)(2,1)S(1)}, bf16[16,1024]{1,0:T(8,128)(2,1)S(1)}, u32[]{:S(2)}, u32[]{:S(2)}) collective-permute-start(bf16[16,1024]{1,0:T(8,128)(2,1)S(1)} %get-tuple-element.15.gate_ref), channel_id=1, source_target_pairs={{0,4},{1,5},{2,6},{3,7},{4,0},{5,1},{6,2},{7,3},{8,12},{9,13},{10,... | collective-permute-start | bytes 98312 | tf_op jit(solution)/shard_map/ppermute | solution.py:420
  9.6 0.8 %copy-start.2 = (f32[16,3,3,3,3]{0,4,3,2,1:T(4,128)S(1)}, f32[16,3,3,3,3]{0,4,3,2,1:T(4,128)}, u32[]{:S(2)}) copy-start(f32[16,3,3,3,3]{0,4,3,2,1:T(4,128)} %param.7) | copy-start | bytes 15556
  10.4 1.0 %copy-start = (bf16[2,128,1024]{2,1,0:T(8,128)(2,1)S(1)}, bf16[2,128,1024]{2,1,0:T(8,128)(2,1)}, u32[]{:S(2)}) copy-start(bf16[2,128,1024]{2,1,0:T(8,128)(2,1)} %target_ref.1) | copy-start | bytes 1572868
  13.7 1.4 %collective-permute-start.4 = (bf16[64,1024]{1,0:T(8,128)(2,1)S(1)}, bf16[64,1024]{1,0:T(8,128)(2,1)S(1)}, u32[]{:S(2)}, u32[]{:S(2)}) collective-permute-start(bf16[64,1024]{1,0:T(8,128)(2,1)S(1)} %constant_dynamic-update-slice_fusion.2.near_ref), channel_id=1, source_target_pairs={{0,1},{1,0},{2,3},{3,2},{4,5},{5,4},{6,7},{7,6},{8,9},{9,8},{10,11... | collective-permute-start | bytes 393224 | tf_op jit(solution)/shard_map/ppermute | solution.py:491

commit v10 on v8

--- a/solution.py
+++ b/solution.py
@@ -412,7 +412,7 @@
     stages = [[2]]
     for first in range(0, len(upper), 2):
         pair = upper[first : first + 2]
-        stages.append(pair if len(pair) == 1 else [pair[0], pair[0] ^ pair[1], pair[1]])
+        stages.append(pair if len(pair) == 1 else [pair[0], pair[1], pair[0] ^ pair[1]])
     masks = [0]
     gate = None
     for stage in stages:

time: 42.1 us -> 42.2 us (level)
  no operation moved by 1% of the time
where the time goes in v10:
time: 42.2 us; the launch traced here: 41.9 us
  blocking collectives  22.1 us (52%)
  starting transfers between devices  7.74 us (18%)
  Pallas kernels  5.63 us (13%)
  waiting for transfers between devices  4.33 us (10%)
  local copies, waits for them, and re-layouts  1.96 us (5%)
    all_to_all x2, blocking collectives, exchange(): return lax.all_to_all(slots, 'tgt', 0, 0, tiled=True)  22.1 us
    ppermute x4, starting transfers between devices, gather_sources(): lax.ppermute(value, 'tgt', [(i, i ^ mask) for i in range(devices)])  7.67 us
    ppermute x4, waiting for transfers between devices, gather_sources(): lax.ppermute(value, 'tgt', [(i, i ^ mask) for i in range(devices)])  3.31 us
    pallas_call x1, Pallas kernels, shards(): pl.pallas_call(functools.partial(consensus_kernel, parts, local, rows), o...  3.16 us
    unnamed x9, local copies, waits for them, and re-layouts  1.95 us
    ppermute x1, waiting for transfers between devices, shards(): far = lax.ppermute(near, 'tgt', [(i, i ^ 1) for i in range(devices)])  1.02 us
    pallas_call x1, Pallas kernels, shards(): pl.pallas_call(functools.partial(finish_kernel, local), out_shape=jax.Sha...  0.86 us
  transfers between devices with their start and end apart: 5, of which 4 were waited for; matrix products, arithmetic and copies ran while one was open for 2% of the time, Pallas kernels for 3%

profile of v10, /device:TPU:0, one launch (start us, length us, event | category | flops | bytes accessed | tf_op | source)
XLA Modules:
  0.0 41.9 jit_solution(6430066493699716314)
XLA Ops:
  0.0 0.0 copy-start.1
  0.0 3.0 %collective-permute-start = (bf16[8,1024]{1,0:T(8,128)(2,1)}, bf16[8,1024]{1,0:T(8,128)(2,1)S(1)}, u32[]{:S(2)}, u32[]{:S(2)}) collective-permute-start(bf16[8,1024]{1,0:T(8,128)(2,1)} %param.4), channel_id=1, source_target_pairs={{0,2},{1,3},{2,0},{3,1},{4,6},{5,7},{6,4},{7,5},{8,10},{9,11},{10,... | collective-permute-start | bytes 49160 | tf_op jit(solution)/shard_map/ppermute | solution.py:420
  3.0 0.8 %constant_dynamic-update-slice_fusion.1 = (bf16[16,1024]{1,0:T(8,128)(2,1)S(1)}, bf16[64,1024]{1,0:T(8,128)(2,1)S(1)}) fusion(bf16[8,1024]{1,0:T(8,128)(2,1)} %param.4), kind=kLoop, calls=%fused_computation.1 | loop fusion | bytes 49152
  3.8 1.2 %collective-permute-done = bf16[8,1024]{1,0:T(8,128)(2,1)S(1)} collective-permute-done((bf16[8,1024]{1,0:T(8,128)(2,1)}, bf16[8,1024]{1,0:T(8,128)(2,1)S(1)}, u32[]{:S(2)}, u32[]{:S(2)}) %collective-permute-start) | collective-permute-done | bytes 16416 | tf_op jit(solution)/shard_map/ppermute | solution.py:420
  4.9 4.1 %collective-permute-start.3 = (bf16[16,1024]{1,0:T(8,128)(2,1)S(1)}, bf16[16,1024]{1,0:T(8,128)(2,1)S(1)}, u32[]{:S(2)}, u32[]{:S(2)}) collective-permute-start(bf16[16,1024]{1,0:T(8,128)(2,1)S(1)} %get-tuple-element.15.gate_ref), channel_id=1, source_target_pairs={{0,12},{1,13},{2,14},{3,15},{4,8},{5,9},{6,10},{7,11},{8,4},{9,5},... | collective-permute-start | bytes 98312 | tf_op jit(solution)/shard_map/ppermute | solution.py:420
  9.0 0.0 collective-permute-start.2
  9.0 0.6 %collective-permute-start.1 = (bf16[16,1024]{1,0:T(8,128)(2,1)S(1)}, bf16[16,1024]{1,0:T(8,128)(2,1)S(1)}, u32[]{:S(2)}, u32[]{:S(2)}) collective-permute-start(bf16[16,1024]{1,0:T(8,128)(2,1)S(1)} %get-tuple-element.15.gate_ref), channel_id=1, source_target_pairs={{0,4},{1,5},{2,6},{3,7},{4,0},{5,1},{6,2},{7,3},{8,12},{9,13},{10,... | collective-permute-start | bytes 98312 | tf_op jit(solution)/shard_map/ppermute | solution.py:420
  9.6 0.0 copy-done.1
  9.6 0.0 copy-start.2
  9.6 0.8 %copy-done.2 = f32[16,3,3,3,3]{0,4,3,2,1:T(4,128)S(1)} copy-done((f32[16,3,3,3,3]{0,4,3,2,1:T(4,128)S(1)}, f32[16,3,3,3,3]{0,4,3,2,1:T(4,128)}, u32[]{:S(2)}) %copy-start.2) | copy-done | bytes 5208
  10.4 0.7 %prepare.1 = (bf16[320,240]{1,0:T(8,128)(2,1)S(1)}, bf16[288,640]{1,0:T(8,128)(2,1)S(1)}) custom-call(f32[3,3,3,3,16]{4,3,2,1,0:T(4,128)S(1)} %bitcast.3, f32[3,3,3,3,16]{4,3,2,1,0:T(4,128)S(1)} %bitcast.4, bf16[16,1024]{1,0:T(8,128)(2,1)S(1)} %get-tuple-element.15.gate_ref), custom_call_target="tpu_custom_call" | custom-call | flops 1000000000 | bytes 1000000 | tf_op jit(solution)/shard_map/prepare/pallas_call | solution.py:461
  11.1 0.4 copy-done
  11.5 0.2 target.1.target_ref
  11.7 1.2 %collective-permute-done.1 = bf16[16,1024]{1,0:T(8,128)(2,1)S(1)} collective-permute-done((bf16[16,1024]{1,0:T(8,128)(2,1)S(1)}, bf16[16,1024]{1,0:T(8,128)(2,1)S(1)}, u32[]{:S(2)}, u32[]{:S(2)}) %collective-permute-start.1) | collective-permute-done | bytes 32800 | tf_op jit(solution)/shard_map/ppermute | solution.py:420
  13.0 0.9 %collective-permute-done.2 = bf16[16,1024]{1,0:T(8,128)(2,1)S(1)} collective-permute-done((bf16[16,1024]{1,0:T(8,128)(2,1)S(1)}, bf16[16,1024]{1,0:T(8,128)(2,1)S(1)}, u32[]{:S(2)}, u32[]{:S(2)}) %collective-permute-start.2) | collective-permute-done | bytes 32800 | tf_op jit(solution)/shard_map/ppermute | solution.py:420
  13.9 0.0 collective-permute-done.3
  13.9 0.1 collective-permute-start.4
  13.9 0.3 near.1.near_ref
  14.3 1.0 %collective-permute-done.4.far_ref = bf16[64,1024]{1,0:T(8,128)(2,1)S(1)} collective-permute-done((bf16[64,1024]{1,0:T(8,128)(2,1)S(1)}, bf16[64,1024]{1,0:T(8,128)(2,1)S(1)}, u32[]{:S(2)}, u32[]{:S(2)}) %collective-permute-start.4) | collective-permute-done | bytes 131104 | tf_op jit(solution)/shard_map/ppermute | solution.py:491
  15.3 0.4 match.1
  15.7 12.1 %all_to_all.10 = f16[16,32,128]{2,1,0:T(8,128)(2,1)S(1)} all-to-all(f16[16,32,128]{2,1,0:T(8,128)(2,1)S(1)} %convert_element_type.12), channel_id=1, replica_groups=mesh['pairs'=2,'tgt'=16] {'tgt'}, dimensions={0} | all-to-all | bytes 262144 | tf_op jit(solution)/shard_map/all_to_all | solution.py:429
  27.8 3.2 %consensus.1 = f32[16,24,128]{2,1,0:T(8,128)S(1)} custom-call(f32[16,32,128]{2,1,0:T(8,128)S(1)} %convert_element_type.13.came_ref, bf16[320,240]{1,0:T(8,128)(2,1)S(1)} %get-tuple-element.13.gate_ref.first_ref, bf16[288,640]{1,0:T(8,128)(2,1)S(1)} %get-tuple-element.14.second_ref), custom_call_target="tpu_custom_call" | custom-call | tf_op jit(solution)/shard_map/consensus/pallas_call | solution.py:519
  31.0 10.0 %all_to_all.11 = f16[16,24,128]{2,1,0:T(8,128)(2,1)S(1)} all-to-all(f16[16,24,128]{2,1,0:T(8,128)(2,1)S(1)} %convert_element_type.14), channel_id=1, replica_groups=mesh['pairs'=2,'tgt'=16] {'tgt'}, dimensions={0} | all-to-all | bytes 196608 | tf_op jit(solution)/shard_map/all_to_all | solution.py:429
  41.0 0.9 %finish.1 = f32[128,2,128]{2,1,0:T(2,128)} custom-call(f32[16,24,128]{2,1,0:T(8,128)S(1)} %convert_element_type.15.came_ref), custom_call_target="tpu_custom_call" | custom-call | tf_op jit(solution)/shard_map/finish/pallas_call | solution.py:529
  (9 shorter events, 0.1 us)
Async XLA Ops:
  0.0 9.6 %copy-start.1 = (f32[16,3,3,3,3]{0,4,3,2,1:T(4,128)S(1)}, f32[16,3,3,3,3]{0,4,3,2,1:T(4,128)}, u32[]{:S(2)}) copy-start(f32[16,3,3,3,3]{0,4,3,2,1:T(4,128)} %param.6) | copy-start | bytes 15556
  0.0 4.9 %collective-permute-start = (bf16[8,1024]{1,0:T(8,128)(2,1)}, bf16[8,1024]{1,0:T(8,128)(2,1)S(1)}, u32[]{:S(2)}, u32[]{:S(2)}) collective-permute-start(bf16[8,1024]{1,0:T(8,128)(2,1)} %param.4), channel_id=1, source_target_pairs={{0,2},{1,3},{2,0},{3,1},{4,6},{5,7},{6,4},{7,5},{8,10},{9,11},{10,... | collective-permute-start | bytes 49160 | tf_op jit(solution)/shard_map/ppermute | solution.py:420
  4.9 8.9 %collective-permute-start.3 = (bf16[16,1024]{1,0:T(8,128)(2,1)S(1)}, bf16[16,1024]{1,0:T(8,128)(2,1)S(1)}, u32[]{:S(2)}, u32[]{:S(2)}) collective-permute-start(bf16[16,1024]{1,0:T(8,128)(2,1)S(1)} %get-tuple-element.15.gate_ref), channel_id=1, source_target_pairs={{0,12},{1,13},{2,14},{3,15},{4,8},{5,9},{6,10},{7,11},{8,4},{9,5},... | collective-permute-start | bytes 98312 | tf_op jit(solution)/shard_map/ppermute | solution.py:420
  9.0 4.8 %collective-permute-start.2 = (bf16[16,1024]{1,0:T(8,128)(2,1)S(1)}, bf16[16,1024]{1,0:T(8,128)(2,1)S(1)}, u32[]{:S(2)}, u32[]{:S(2)}) collective-permute-start(bf16[16,1024]{1,0:T(8,128)(2,1)S(1)} %get-tuple-element.15.gate_ref), channel_id=1, source_target_pairs={{0,8},{1,9},{2,10},{3,11},{4,12},{5,13},{6,14},{7,15},{8,0},{9,1},... | collective-permute-start | bytes 98312 | tf_op jit(solution)/shard_map/ppermute | solution.py:420
  9.0 3.9 %collective-permute-start.1 = (bf16[16,1024]{1,0:T(8,128)(2,1)S(1)}, bf16[16,1024]{1,0:T(8,128)(2,1)S(1)}, u32[]{:S(2)}, u32[]{:S(2)}) collective-permute-start(bf16[16,1024]{1,0:T(8,128)(2,1)S(1)} %get-tuple-element.15.gate_ref), channel_id=1, source_target_pairs={{0,4},{1,5},{2,6},{3,7},{4,0},{5,1},{6,2},{7,3},{8,12},{9,13},{10,... | collective-permute-start | bytes 98312 | tf_op jit(solution)/shard_map/ppermute | solution.py:420
  9.6 0.8 %copy-start.2 = (f32[16,3,3,3,3]{0,4,3,2,1:T(4,128)S(1)}, f32[16,3,3,3,3]{0,4,3,2,1:T(4,128)}, u32[]{:S(2)}) copy-start(f32[16,3,3,3,3]{0,4,3,2,1:T(4,128)} %param.7) | copy-start | bytes 15556
  10.4 1.0 %copy-start = (bf16[2,128,1024]{2,1,0:T(8,128)(2,1)S(1)}, bf16[2,128,1024]{2,1,0:T(8,128)(2,1)}, u32[]{:S(2)}) copy-start(bf16[2,128,1024]{2,1,0:T(8,128)(2,1)} %target_ref.1) | copy-start | bytes 1572868
  13.9 1.4 %collective-permute-start.4 = (bf16[64,1024]{1,0:T(8,128)(2,1)S(1)}, bf16[64,1024]{1,0:T(8,128)(2,1)S(1)}, u32[]{:S(2)}, u32[]{:S(2)}) collective-permute-start(bf16[64,1024]{1,0:T(8,128)(2,1)S(1)} %constant_dynamic-update-slice_fusion.2.near_ref), channel_id=1, source_target_pairs={{0,1},{1,0},{2,3},{3,2},{4,5},{5,4},{6,7},{7,6},{8,9},{9,8},{10,11... | collective-permute-start | bytes 393224 | tf_op jit(solution)/shard_map/ppermute | solution.py:491
